TPU v7x, 512 devices: a whole 4x4x16 slice. The times are simulated.
512 devices in a mesh: dp: 8 (over x_hi, y), ctx: 64 (over z, x_lo, core).
Axes of the slice: x: 4 (x_hi: 2, x_lo: 2; x = x_hi * 2 + x_lo), y: 4, z: 16, core: 2. Of those that a mesh axis runs over, the one named last changes fastest.
Arguments:
- embeds: bfloat16 [8, 65536, 128], P('dp', 'ctx'), may hold values from -6 to 6
- perturb: bfloat16 [8, 65536, 128], P('dp', 'ctx'), may hold values from -1.5 to 1.5
- cotangent: bfloat16 [8, 65536, 128], P('dp', 'ctx'), may hold values from -6 to 6
- filter_spectrum: float32 [2, 256, 256, 128], P(None, 'ctx'), may hold values from -4.2 to 4.2
- skip_gain: float32 [128], replicated, may hold values from 0.25 to 1.75
Outputs:
- clean_output: bfloat16 [8, 65536, 128], P('dp', 'ctx')
- filter_grad: float32 [2, 256, 256, 128], P(None, 'ctx', 'dp')
All inputs are finite; a program needn't handle non-finite values.
Results may differ from a plain program's by a relative error of at most 0.022.
Values may be sent and summed in bfloat16 or wider, within the bound.
A program may use at most 64 MiB of HBM per device.

v0:
```python
import jax
import jax.numpy as jnp
from jax import lax
from jax.sharding import PartitionSpec as P

N1 = 256
N2 = 256


two_pi = 6.283185307179586
smart_weight = 2.0


def trig_table(period):
    row_ids = jnp.arange(period, dtype=jnp.int32)
    exponent = row_ids[:, None] * row_ids[None, :] % period
    phase_angle = exponent.astype(jnp.float32) * (two_pi / period)
    return (jnp.cos(phase_angle).astype(jnp.bfloat16), jnp.sin(phase_angle).astype(jnp.bfloat16))


def twiddle(row_first, row_count, col_first, col_count):
    row_ids = row_first + jnp.arange(row_count, dtype=jnp.int32)
    col_ids = col_first + jnp.arange(col_count, dtype=jnp.int32)
    exponent = row_ids[:, None] * col_ids[None, :] % (N1 * N2)
    phase_angle = exponent.astype(jnp.float32) * (two_pi / (N1 * N2))
    return (jnp.cos(phase_angle)[:, :, None], jnp.sin(phase_angle)[:, :, None])


def first_section(values, col_start):
    cos_table, sin_table = trig_table(N1)
    part_real = jnp.einsum("kn,snmc->skmc", cos_table, values, preferred_element_type=jnp.float32)
    part_imag = -jnp.einsum("kn,snmc->skmc", sin_table, values, preferred_element_type=jnp.float32)
    tw_cos, tw_sin = twiddle(0, N1, col_start, values.shape[2])
    out_real = part_real * tw_cos + part_imag * tw_sin
    out_imag = part_imag * tw_cos - part_real * tw_sin
    return jnp.stack([out_real, out_imag], 1).astype(jnp.bfloat16)


def second_section(section_rows):
    cos_table, sin_table = trig_table(N2)
    with_cos = jnp.einsum(
        "sprnc,kn->sprkc", section_rows, cos_table, preferred_element_type=jnp.float32
    )
    with_sin = jnp.einsum(
        "sprnc,kn->sprkc", section_rows, sin_table, preferred_element_type=jnp.float32
    )
    return jnp.stack([with_cos[:, 0] + with_sin[:, 1], with_cos[:, 1] - with_sin[:, 0]], 1)


def spectral_inverse(product, row_start):
    cos_table, sin_table = trig_table(N2)
    with_cos = jnp.einsum("sprkc,nk->sprnc", product, cos_table, preferred_element_type=jnp.float32)
    with_sin = jnp.einsum("sprkc,nk->sprnc", product, sin_table, preferred_element_type=jnp.float32)
    part_real = with_cos[:, 0] - with_sin[:, 1]
    part_imag = with_cos[:, 1] + with_sin[:, 0]
    tw_cos, tw_sin = twiddle(row_start, product.shape[2], 0, N2)
    out_real = part_real * tw_cos - part_imag * tw_sin
    out_imag = part_imag * tw_cos + part_real * tw_sin
    return jnp.stack([out_real, out_imag], 1).astype(jnp.bfloat16)


def column_inverse(mixed_cols):
    cos_table, sin_table = trig_table(N1)
    with_cos = jnp.einsum(
        "nk,skmc->snmc", cos_table, mixed_cols[:, 0], preferred_element_type=jnp.float32
    )
    with_sin = jnp.einsum(
        "nk,skmc->snmc", sin_table, mixed_cols[:, 1], preferred_element_type=jnp.float32
    )
    return ((with_cos - with_sin) * (1.0 / (N1 * N2))).astype(jnp.bfloat16)


def to_spectrum(section_cols):
    return second_section(
        lax.all_to_all(section_cols, "ctx", split_axis=2, concat_axis=3, tiled=True)
    )


def error_terms(signal, filtered, skip_gain, cotangent_view):
    signal_wide = signal.astype(jnp.float32)
    filtered_wide = lax.optimization_barrier(filtered).astype(jnp.float32)
    outputs = signal_wide * filtered_wide + skip_gain * signal_wide
    clean_y = outputs[0]
    smooth_gap = outputs[1] - clean_y
    err_clean = signal_wide[0] * (cotangent_view.astype(jnp.float32) - smart_weight * smooth_gap)
    err_shift = signal_wide[1] * (smart_weight * smooth_gap)
    return (clean_y, jnp.stack([err_clean, err_shift], 0).astype(jnp.bfloat16))


def body(embeds, perturb, cotangent, filter_spectrum, skip_gain):
    ctx_size = lax.axis_size("ctx")
    ctx_index = lax.axis_index("ctx")
    channels = embeds.shape[2]
    row_count = N1 // ctx_size
    col_count = N2 // ctx_size
    row_start = ctx_index * row_count
    col_start = ctx_index * col_count
    clean_rows = embeds[0].reshape(row_count, N2, channels)
    perturb_rows = perturb[0].reshape(row_count, N2, channels)
    shifted = (clean_rows.astype(jnp.float32) + perturb_rows.astype(jnp.float32)).astype(
        jnp.bfloat16
    )
    inputs = jnp.stack([clean_rows, shifted], 0)
    signal_cols = lax.all_to_all(inputs, "ctx", split_axis=2, concat_axis=1, tiled=True)
    section_cols, signal_cols = (first_section(signal_cols, col_start), signal_cols)
    spectra = to_spectrum(section_cols)
    filter_real = filter_spectrum[0]
    filter_imag = filter_spectrum[1]
    spectrum_real = spectra[:, 0]
    spectrum_imag = spectra[:, 1]
    product = jnp.stack(
        [
            filter_real * spectrum_real - filter_imag * spectrum_imag,
            filter_real * spectrum_imag + filter_imag * spectrum_real,
        ],
        1,
    ).astype(jnp.bfloat16)
    mixed_rows = spectral_inverse(product, row_start)
    filtered = column_inverse(
        lax.all_to_all(mixed_rows, "ctx", split_axis=3, concat_axis=2, tiled=True)
    )
    cotangent_rows = cotangent[0].reshape(row_count, N2, channels)
    filtered_rows = lax.all_to_all(filtered, "ctx", split_axis=1, concat_axis=2, tiled=True)
    clean_y, errors = error_terms(inputs, filtered_rows, skip_gain, cotangent_rows)
    clean_output = clean_y.astype(jnp.bfloat16)
    error_section = first_section(
        lax.all_to_all(errors, "ctx", split_axis=2, concat_axis=1, tiled=True), col_start
    )
    error_spec = to_spectrum(error_section)
    error_real = error_spec[:, 0]
    error_imag = error_spec[:, 1]
    term_real = error_real * spectrum_real + error_imag * spectrum_imag
    term_imag = error_imag * spectrum_real - error_real * spectrum_imag
    local_grad = jnp.stack([term_real[0] + term_real[1], term_imag[0] + term_imag[1]], 0) * (
        1.0 / (N1 * N2)
    )
    grad_shard = lax.psum_scatter(
        local_grad.astype(jnp.bfloat16), "dp", scatter_dimension=2, tiled=True
    ).astype(jnp.float32)
    return (clean_output.reshape(1, row_count * N2, channels), grad_shard)


def solution(mesh):
    return jax.shard_map(
        body,
        mesh=mesh,
        in_specs=(
            P("dp", "ctx", None),
            P("dp", "ctx", None),
            P("dp", "ctx", None),
            P(None, "ctx", None, None),
            P(),
        ),
        out_specs=(P("dp", "ctx", None), P(None, "ctx", "dp", None)),
        check_vma=False,
    )
```

profile of v0, /device:TPU:1, one launch (start us, length us, event | category | flops | bytes accessed | tf_op | source)
XLA Modules:
  0.0 435.0 jit_solution(4383637217935503751)
XLA Ops:
  7.2 1.1 fusion.16
  8.3 0.7 copy-done.2
  9.0 2.1 fusion.95
  11.0 1.2 copy.25
  12.2 18.1 %all-to-all-start = ((bf16[2,4,256,128]{3,1,0,2:T(4,128)(2,1)}), bf16[2,4,256,128]{3,1,0,2:T(4,128)(2,1)S(1)}, u32[]{:S(2)}, u32[]{:S(2)}) async-start(bf16[2,4,256,128]{3,1,0,2:T(4,128)(2,1)} %copy.25), calls=%async_computation | async-start | bytes 1048576 | tf_op jit(solution)/shard_map/all_to_all | solution.py:104
  30.5 32.4 %all-to-all-done = bf16[2,4,256,128]{3,1,0,2:T(4,128)(2,1)S(1)} async-done(((bf16[2,4,256,128]{3,1,0,2:T(4,128)(2,1)}), bf16[2,4,256,128]{3,1,0,2:T(4,128)(2,1)S(1)}, u32[]{:S(2)}, u32[]{:S(2)}) %all-to-all-start) | async-done | bytes 524320 | tf_op jit(solution)/shard_map/all_to_all | solution.py:104
  62.9 0.4 copy.27
  63.3 1.2 fusion.2
  64.6 1.3 fusion.6
  66.1 1.8 copy.30
  67.9 5.7 %all-to-all-start.1 = ((bf16[2,2,256,4,128]{4,3,0,1,2:T(4,128)(2,1)}), bf16[2,2,256,4,128]{4,3,0,1,2:T(4,128)(2,1)S(1)}, u32[]{:S(2)}, u32[]{:S(2)}) async-start(bf16[2,2,256,4,128]{4,3,0,1,2:T(4,128)(2,1)} %copy.30), calls=%async_computation.1 | async-start | bytes 2097152 | tf_op jit(solution)/shard_map/all_to_all | solution.py:75
  73.6 0.2 reduce-scatter.2.cloned.1.call-start
  74.0 53.6 %all-to-all-done.1 = bf16[2,2,256,4,128]{4,3,0,1,2:T(4,128)(2,1)S(1)} async-done(((bf16[2,2,256,4,128]{4,3,0,1,2:T(4,128)(2,1)}), bf16[2,2,256,4,128]{4,3,0,1,2:T(4,128)(2,1)S(1)}, u32[]{:S(2)}, u32[]{:S(2)}) %all-to-all-start.1) | async-done | bytes 1048608 | tf_op jit(solution)/shard_map/all_to_all | solution.py:75
  127.6 0.3 copy.31
  127.9 0.8 copy.32
  128.7 1.3 convolution_bitcast_fusion.4
  130.0 1.3 convolution_bitcast_fusion.5
  131.3 0.4 subtract_convert_fusion.2
  131.7 0.2 add_convert_fusion.2
  131.9 1.3 convolution_bitcast_fusion.2
  133.2 1.3 convolution_bitcast_fusion.3
  134.6 0.5 subtract_convert_fusion.1
  135.2 0.8 copy.33
  136.0 60.0 %all_to_all.108 = bf16[2,2,4,256,128]{4,2,1,0,3:T(4,128)(2,1)S(1)} all-to-all(bf16[2,2,4,256,128]{4,2,1,0,3:T(4,128)(2,1)S(1)} %copy.33), channel_id=1, replica_groups=mesh['dp'=8,'ctx'=64] {'ctx'}, dimensions={3} | all-to-all | bytes 2097152 | tf_op jit(solution)/shard_map/all_to_all | solution.py:120
  196.0 0.5 copy.34
  196.5 1.2 fusion.15
  197.7 1.2 fusion.4
  199.0 0.3 copy.37
  199.3 39.2 %all_to_all.109 = bf16[2,256,4,128]{3,2,0,1:T(4,128)(2,1)S(1)} all-to-all(bf16[2,256,4,128]{3,2,0,1:T(4,128)(2,1)S(1)} %copy.37), channel_id=1, replica_groups=mesh['dp'=8,'ctx'=64] {'ctx'}, dimensions={1} | all-to-all | bytes 1048576 | tf_op jit(solution)/shard_map/all_to_all | solution.py:123
  238.6 0.4 copy.39
  239.2 0.6 copy-done
  240.0 0.4 copy.40
  240.4 37.5 %all_to_all.110 = bf16[2,4,256,128]{3,1,0,2:T(4,128)(2,1)S(1)} all-to-all(bf16[2,4,256,128]{3,1,0,2:T(4,128)(2,1)S(1)} %copy.40), channel_id=1, replica_groups=mesh['dp'=8,'ctx'=64] {'ctx'}, dimensions={2} | all-to-all | bytes 1048576 | tf_op jit(solution)/shard_map/all_to_all | solution.py:127
  278.0 0.4 copy.42
  278.4 1.2 fusion
  279.7 1.3 fusion.8
  281.0 1.1 pad_maximum_fusion.3
  282.1 2.7 copy.45
  284.8 59.3 %all_to_all.111 = bf16[2,2,256,4,128]{4,3,0,1,2:T(4,128)(2,1)S(1)} all-to-all(bf16[2,2,256,4,128]{4,3,0,1,2:T(4,128)(2,1)} %copy.45), channel_id=1, replica_groups=mesh['dp'=8,'ctx'=64] {'ctx'}, dimensions={2} | all-to-all | bytes 2097152 | tf_op jit(solution)/shard_map/all_to_all | solution.py:75
  344.1 0.3 copy.46
  344.4 0.8 copy.47
  345.2 1.3 convolution_bitcast_fusion
  346.5 1.3 convolution_bitcast_fusion.1
  347.9 0.5 multiply_add_fusion
  348.5 0.9 fusion.5
  349.4 0.7 slice.199
  350.1 76.5 %reduce-scatter.2.cloned.1.call-done = bf16[2,4,32,128]{3,2,1,0:T(8,128)(2,1)} async-done(((bf16[2,4,256,128]{3,2,1,0:T(8,128)(2,1)}), bf16[2,4,32,128]{3,2,1,0:T(8,128)(2,1)}) %reduce-scatter.2.cloned.1.call-update) | async-done | bytes 65552 | tf_op jit(solution)/shard_map/reduce_scatter | solution.py:137
  426.6 1.5 convert_element_type.187
  (26 shorter events, 1.3 us)
Async XLA Ops:
  8.3 0.7 copy-start.2
  12.2 50.6 %all-to-all-start = ((bf16[2,4,256,128]{3,1,0,2:T(4,128)(2,1)}), bf16[2,4,256,128]{3,1,0,2:T(4,128)(2,1)S(1)}, u32[]{:S(2)}, u32[]{:S(2)}) async-start(bf16[2,4,256,128]{3,1,0,2:T(4,128)(2,1)} %copy.25), calls=%async_computation | async-start | bytes 1048576 | tf_op jit(solution)/shard_map/all_to_all | solution.py:104
  66.1 7.9 %copy-start.4 = (f32[2,4,256,128]{3,2,1,0:T(8,128)S(1)}, f32[2,4,256,128]{3,2,1,0:T(8,128)}, u32[]{:S(2)}) copy-start(f32[2,4,256,128]{3,2,1,0:T(8,128)} %param.8) | copy-start | bytes 3145732
  67.9 59.7 %all-to-all-start.1 = ((bf16[2,2,256,4,128]{4,3,0,1,2:T(4,128)(2,1)}), bf16[2,2,256,4,128]{4,3,0,1,2:T(4,128)(2,1)S(1)}, u32[]{:S(2)}, u32[]{:S(2)}) async-start(bf16[2,2,256,4,128]{4,3,0,1,2:T(4,128)(2,1)} %copy.30), calls=%async_computation.1 | async-start | bytes 2097152 | tf_op jit(solution)/shard_map/all_to_all | solution.py:75
  73.6 353.0 %reduce-scatter.2.cloned.1.call-start = ((), (), s32[]{:S(2)}) async-start(), calls=%async_computation.7 | async-start | bytes 589824 | tf_op jit(solution)/shard_map/reduce_scatter | solution.py:137
  199.0 40.0 %copy-start.1 = (bf16[1,1024,128]{2,1,0:T(8,128)(2,1)S(1)}, bf16[1,1024,128]{2,1,0:T(8,128)(2,1)}, u32[]{:S(2)}) copy-start(bf16[1,1024,128]{2,1,0:T(8,128)(2,1)} %param.5) | copy-start | bytes 786436
  199.0 40.0 %copy-start.6 = (f32[128]{0:T(128)S(1)}, f32[128]{0:T(128)}, u32[]{:S(2)}) copy-start(f32[128]{0:T(128)} %param.9) | copy-start | bytes 1540
  199.3 39.7 %copy-start.3 = (bf16[1,4,256,128]{3,2,1,0:T(8,128)(2,1)S(1)}, bf16[1,4,256,128]{3,2,1,0:T(8,128)(2,1)}, u32[]{:S(2)}) copy-start(bf16[1,4,256,128]{3,2,1,0:T(8,128)(2,1)} %copy-done.2) | copy-start | bytes 786436
  238.5 1.2 copy-start
  238.5 1.3 copy-start.5
Sparse Core Ops, SparseCore 0:
  349.5 77.0 reduce-scatter.1
where the time goes:
time: 436 us; the launch traced here: 435 us
  blocking collectives  196 us (45%)
  waiting for transfers between devices  162 us (37%)
  starting transfers between devices  24 us (6%)
  matrix products  15.6 us (4%)
  between operations  14.4 us (3%)
  local copies, waits for them, and re-layouts  13.4 us (3%)
  other arithmetic  9.08 us (2%)
    reduce_scatter x1, waiting for transfers between devices, body(): lax.psum_scatter(local_grad.astype(jnp.bfloat16), 'dp', scatter_dimension...  76.5 us
    all_to_all x1, blocking collectives, body(): lax.all_to_all(mixed_rows, 'ctx', split_axis=3, concat_axis=2, tiled=True)  60 us
    all_to_all x1, blocking collectives, to_spectrum(): lax.all_to_all(section_cols, 'ctx', split_axis=2, concat_axis=3, tiled=True)  59.3 us
    all_to_all x1, waiting for transfers between devices, to_spectrum(): lax.all_to_all(section_cols, 'ctx', split_axis=2, concat_axis=3, tiled=True)  53.6 us
    all_to_all x1, blocking collectives, body(): lax.all_to_all(filtered, 'ctx', split_axis=1, concat_axis=2, tiled=True)  39.2 us
    all_to_all x1, blocking collectives, body(): lax.all_to_all(errors, 'ctx', split_axis=2, concat_axis=1, tiled=True)  37.5 us
    all_to_all x1, waiting for transfers between devices, body(): lax.all_to_all(inputs, 'ctx', split_axis=2, concat_axis=1, tiled=True)  32.4 us
    all_to_all x1, starting transfers between devices, body(): lax.all_to_all(inputs, 'ctx', split_axis=2, concat_axis=1, tiled=True)  18.1 us
  transfers between devices with their start and end apart: 3, of which 3 were waited for; matrix products, arithmetic and copies ran while one was open for 0% of the time, Pallas kernels for 0%

commit v1 on v0

v1 whole, which is shorter than its diff:
```python
import numpy as np
import jax
import jax.numpy as jnp
from jax import lax
from jax.sharding import PartitionSpec as P

M1 = 512
M2 = 128
N = M1 * M2
SMART = 2.0
BF = jnp.bfloat16
F32 = jnp.float32


def trig(rows, cols, period):
    turn = (np.arange(rows)[:, None] * np.arange(cols)[None, :]) % period
    angle = turn * (2.0 * np.pi / period)
    return np.cos(angle), np.sin(angle)


def tables():
    c1, s1 = trig(M1, M1, M1)
    tc, ts = trig(M1, M2, N)
    c2, s2 = trig(M2, M2, M2)
    wf = np.block([[c2, s2], [-s2, c2]])
    wi = np.block([[c2, -s2], [s2, c2]])
    return c1, s1, tc, ts, wf, wi


def dot(a, b, ca, cb):
    return lax.dot_general(a, b, (((ca,), (cb,)), ((), ())), preferred_element_type=F32)


def forward(x, tabs):
    c1, s1, tc, ts, wf, wi = tabs
    ar = dot(c1, x, 1, 0)
    ai = -dot(s1, x, 1, 0)
    tr = (ar * tc + ai * ts).astype(BF)
    ti = (ai * tc - ar * ts).astype(BF)
    return dot(wf, jnp.concatenate([tr, ti], 1), 1, 1)


def convolve(spec, fr, fi, tabs):
    c1, s1, tc, ts, wf, wi = tabs
    re, im = spec[:M2], spec[M2:]
    prod = jnp.concatenate([fr * re - fi * im, fr * im + fi * re], 0).astype(BF)
    v = dot(wi, prod, 1, 0)
    vr, vi = v[:M2], v[M2:]
    sr = (vr * tc.T - vi * ts.T).astype(BF)
    si = (vi * tc.T + vr * ts.T).astype(BF)
    return ((dot(c1, sr, 1, 1) - dot(s1, si, 1, 1)) * (1.0 / N)).astype(BF)


def grad_term(err, spec):
    er, ei, re, im = err[:M2], err[M2:], spec[:M2], spec[M2:]
    return jnp.concatenate([er * re + ei * im, ei * re - er * im], 0)


def channel_work(e, s, c, filt, gain, tabs):
    fr, fi = filt[:M2].astype(F32), filt[M2:].astype(F32)
    ce = forward(e, tabs)
    cs = forward(s, tabs)
    ef, sf = e.astype(F32), s.astype(F32)
    ye = ef * convolve(ce, fr, fi, tabs).astype(F32) + gain * ef
    ys = sf * convolve(cs, fr, fi, tabs).astype(F32) + gain * sf
    gap = ys - ye
    ee = (ef * (c.astype(F32) - SMART * gap)).astype(BF)
    es = (sf * (SMART * gap)).astype(BF)
    g = grad_term(forward(ee, tabs), ce) + grad_term(forward(es, tabs), cs)
    return ye.astype(BF), (g * (1.0 / N)).astype(BF)


def a2a(x, axis):
    return lax.all_to_all(x, axis, split_axis=0, concat_axis=0, tiled=True)


def body(embeds, perturb, cotangent, filter_spectrum, skip_gain):
    tabs = tables()
    cast = (BF, BF, F32, F32, BF, BF)
    tabs = tuple(jnp.asarray(t.astype(np.float32)).astype(k) for t, k in zip(tabs, cast))
    d = lax.axis_index("dp")
    q = lax.axis_index("ctx")
    e = embeds[0]
    s = (e.astype(F32) + perturb[0].astype(F32)).astype(BF)
    sig = jnp.stack([e, s, cotangent[0]], 0).reshape(3, 8, 128, 64, 2)
    sig = a2a(sig.transpose(3, 0, 4, 1, 2), "ctx")
    sig = sig.transpose(1, 2, 0, 3, 4).reshape(3, 2, M1, M2)
    part = lax.dynamic_slice_in_dim(filter_spectrum, d * 32, 32, 2).astype(BF)
    part = part.reshape(2, 4, 16, 2, 64, 2).transpose(4, 1, 3, 5, 0, 2).reshape(64, 4, 128)
    part = a2a(part, "ctx").reshape(256, 2, 2, 2, 16).transpose(2, 3, 4, 1, 0).reshape(2, 2, 16, M1)
    filt = lax.all_gather(part, "dp", axis=2).reshape(2, 2 * M2, M1)
    gains = lax.dynamic_slice_in_dim(skip_gain, 2 * q, 2, 0)
    ys, gs = [], []
    for j in range(2):
        y, g = channel_work(sig[0, j], sig[1, j], sig[2, j], filt[j], gains[j], tabs)
        ys.append(y.reshape(64, 8, 128))
        gs.append(g.reshape(2, 8, 16, M1))
    out = a2a(jnp.stack(ys, 1), "ctx")
    out = out.transpose(2, 3, 0, 1).reshape(1, 1024, 128)
    g = a2a(jnp.stack(gs, 0).transpose(2, 0, 1, 3, 4), "dp")
    g = g.astype(F32).sum(0).reshape(2, 2, 16, 2, 256).transpose(4, 3, 0, 1, 2)
    g = a2a(g.reshape(64, 4, 128).astype(BF), "ctx").reshape(64, 4, 2, 2, 2, 16)
    g = g.transpose(4, 1, 5, 2, 0, 3).reshape(2, 4, 32, 128).astype(F32)
    return out, g


def solution(mesh):
    return jax.shard_map(
        body,
        mesh=mesh,
        in_specs=(
            P("dp", "ctx", None),
            P("dp", "ctx", None),
            P("dp", "ctx", None),
            P(None, "ctx", None, None),
            P(),
        ),
        out_specs=(P("dp", "ctx", None), P(None, "ctx", "dp", None)),
        check_vma=False,
    )
```

time: 436 us -> 211 us (0.48)
  blocking collectives: 196 us -> 47.9 us
  waiting for transfers between devices: 162 us -> 46.1 us
  local copies, waits for them, and re-layouts: 13.4 us -> 38.1 us
  matrix products: 15.6 us -> 36.4 us
  starting transfers between devices: 24 us -> 37.8 us
  between operations: 14.4 us -> 1.54 us
  other arithmetic: 9.08 us -> 1.97 us
    all_to_all x4 -> x1, blocking collectives: 196 us -> 15.3 us  [a2a(): return lax.all_to_all(x, axis, split_axis=0, concat_axis=0, tiled=True)]
    reduce_scatter x1 -> x0, waiting for transfers between devices: 76.5 us -> none  [body(): lax.psum_scatter(local_grad.astype(jnp.bfloat16), 'dp', scatter_dimension...]
    all_to_all x2 -> x4, waiting for transfers between devices: 85.9 us -> 46.1 us  [a2a(): return lax.all_to_all(x, axis, split_axis=0, concat_axis=0, tiled=True)]
    all_gather x0 -> x1, blocking collectives: none -> 32.6 us  [body(): filt = lax.all_gather(part, 'dp', axis=2).reshape(2, 2 * M2, M1)]
    dot_general x12 -> x48, matrix products: 15.6 us -> 36.4 us  [dot(): lax.dot_general(a, b, (((ca,), (cb,)), ((), ())), preferred_element_type=...]
    unnamed x14 -> x95, local copies, waits for them, and re-layouts: 1.32 us -> 21.3 us
    all_to_all x2 -> x4, starting transfers between devices: 23.8 us -> 37.8 us  [a2a(): return lax.all_to_all(x, axis, split_axis=0, concat_axis=0, tiled=True)]
    convert_element_type x1 -> x10, local copies, waits for them, and re-layouts: 0.31 us -> 7.55 us  [the longest x2 4.64 us: body(): g = g.transpose(4, 1, 5, 2, 0, 3).reshape(2, 4, 32, 128).astype(F32)]
  transfers between devices with their start and end apart: 3 -> 4, of which waited for: 3 -> 4; matrix products, arithmetic and copies ran while one was open for 0% -> 7% of each run, Pallas kernels for 0% -> 0%
where the time goes in v1:
time: 211 us; the launch traced here: 210 us
  blocking collectives  47.9 us (23%)
  waiting for transfers between devices  46.1 us (22%)
  local copies, waits for them, and re-layouts  38.1 us (18%)
  starting transfers between devices  37.8 us (18%)
  matrix products  36.4 us (17%)
    all_to_all x4, waiting for transfers between devices, a2a(): return lax.all_to_all(x, axis, split_axis=0, concat_axis=0, tiled=True)  46.1 us
    all_to_all x4, starting transfers between devices, a2a(): return lax.all_to_all(x, axis, split_axis=0, concat_axis=0, tiled=True)  37.8 us
    dot_general x48, matrix products, dot(): lax.dot_general(a, b, (((ca,), (cb,)), ((), ())), preferred_element_type=...  36.4 us
    all_gather x1, blocking collectives, body(): filt = lax.all_gather(part, 'dp', axis=2).reshape(2, 2 * M2, M1)  32.6 us
    unnamed x95, local copies, waits for them, and re-layouts  21.3 us
    all_to_all x1, blocking collectives, a2a(): return lax.all_to_all(x, axis, split_axis=0, concat_axis=0, tiled=True)  15.3 us
    convert_element_type x2, local copies, waits for them, and re-layouts, body(): g = g.transpose(4, 1, 5, 2, 0, 3).reshape(2, 4, 32, 128).astype(F32)  4.64 us
  transfers between devices with their start and end apart: 4, of which 4 were waited for; matrix products, arithmetic and copies ran while one was open for 7% of the time, Pallas kernels for 0%

profile of v1, /device:TPU:1, one launch (start us, length us, event | category | flops | bytes accessed | tf_op | source)
XLA Modules:
  0.0 209.8 jit_solution(14086083531331770005)
XLA Ops:
  0.7 1.2 copy-done
  1.9 1.1 copy.190
  3.0 1.9 copy.191
  5.6 18.1 %all-to-all-start.1 = ((bf16[64,4,128]{2,1,0:T(4,128)(2,1)}), bf16[64,4,128]{2,1,0:T(4,128)(2,1)S(1)}, u32[]{:S(2)}, u32[]{:S(2)}) async-start(bf16[64,4,128]{2,1,0:T(4,128)(2,1)} %copy.192), calls=%async_computation.1 | async-start | bytes 131072 | tf_op jit(solution)/shard_map/all_to_all | solution.py:74
  23.8 1.0 add_convert_fusion
  25.1 1.1 copy.196
  26.4 1.0 copy.197
  27.4 10.7 %all-to-all-done.1 = bf16[64,4,128]{2,1,0:T(4,128)(2,1)S(1)} async-done(((bf16[64,4,128]{2,1,0:T(4,128)(2,1)}), bf16[64,4,128]{2,1,0:T(4,128)(2,1)S(1)}, u32[]{:S(2)}, u32[]{:S(2)}) %all-to-all-start.1) | async-done | bytes 65568 | tf_op jit(solution)/shard_map/all_to_all | solution.py:74
  38.1 5.2 %all-to-all-start = ((bf16[64,3,2,8,128]{4,3,2,1,0:T(8,128)(2,1)}), bf16[64,3,2,8,128]{4,3,2,1,0:T(8,128)(2,1)}, u32[]{:S(2)}, u32[]{:S(2)}) async-start(bf16[64,3,2,8,128]{4,3,2,1,0:T(8,128)(2,1)} %copy.197), calls=%async_computation | async-start | bytes 1572864 | tf_op jit(solution)/shard_map/all_to_all | solution.py:74
  45.3 32.6 %all_gather.3 = bf16[2,2,8,16,512]{4,3,1,0,2:T(8,128)(2,1)S(1)} all-gather(bf16[2,2,1,16,512]{4,3,1,0,2:T(8,128)(2,1)S(1)} %all_gather_reshape.3), channel_id=1, replica_groups=mesh['dp'=8,'ctx'=64] {'dp'}, dimensions={2}, use_global_device_ids=true | all-gather | bytes 589824 | tf_op jit(solution)/shard_map/all_gather | solution.py:91
  78.7 7.8 %all-to-all-done = bf16[64,3,2,8,128]{4,3,2,1,0:T(8,128)(2,1)} async-done(((bf16[64,3,2,8,128]{4,3,2,1,0:T(8,128)(2,1)}), bf16[64,3,2,8,128]{4,3,2,1,0:T(8,128)(2,1)}, u32[]{:S(2)}, u32[]{:S(2)}) %all-to-all-start) | async-done | bytes 786464 | tf_op jit(solution)/shard_map/all_to_all | solution.py:74
  86.5 1.3 copy.261
  87.8 0.9 fusion.128
  88.9 1.0 convolution_negate_fusion.1
  90.2 1.0 fusion.108
  93.7 1.1 fusion.116
  94.7 1.6 copy.249
  96.4 1.3 fusion.74
  97.7 1.3 convolution_add_fusion.7
  99.0 1.5 fusion.99
  101.6 1.0 fusion.118
  102.6 1.7 copy.251
  104.3 1.7 copy.252
  106.0 2.8 %fusion.132 = (bf16[512,128]{0,1:T(8,128)(2,1)}, f32[512,128]{0,1:T(8,128)S(1)}) fusion(bf16[1,1,512,128]{2,3,1,0:T(8,128)(2,1)} %copy.249, f32[]{:T(128)} %bitcast.14, f32[128,512]{1,0:T(8,128)} %fusion.116, bf16[512,512]{1,0:T(8,128)(2,1)S(1)} %copy-done.2, f32[128,512]{0,1:T(8,128)S(1)} %copy-done.4, f32[128,512]{0,1:T(8,128)S(1)} %copy-done.3, ...), kind=kOutput, calls=%fused_computation.196 | convolution fusion | flops 67895296 | bytes 2359300 | tf_op jit(solution)/shard_map/dot_general | solution.py:31
  108.7 2.2 %fusion.34 = (bf16[512,128]{0,1:T(8,128)(2,1)S(1)}, bf16[512,128]{0,1:T(8,128)(2,1)S(1)}) fusion(bf16[1,1,512,128]{2,3,1,0:T(8,128)(2,1)} %copy.252, bf16[1,1,512,128]{2,3,1,0:T(8,128)(2,1)} %copy.251, bf16[1,1,512,128]{2,3,1,0:T(8,128)(2,1)} %copy.249, f32[512,128]{0,1:T(8,128)S(1)} %get-tuple-element.39, f32[]{:T(128)} %bitcast.14, ...), kind=kOutput, calls=%fused_computation.85 | convolution fusion | flops 68419584 | bytes 2752516 | tf_op jit(solution)/shard_map/dot_general | solution.py:31
  111.0 1.0 convolution_negate_fusion.7
  112.0 1.0 fusion.133
  113.0 1.0 convolution_negate_fusion.6
  114.0 1.0 fusion.134
  115.6 1.0 convolution_negate_fusion
  116.6 1.0 fusion.105
  119.9 1.0 fusion.117
  121.0 1.7 copy.250
  122.7 1.3 fusion.83
  124.0 1.3 convolution_add_fusion.3
  125.3 1.2 fusion.93
  127.9 1.7 copy.253
  129.5 1.7 copy.254
  131.2 2.9 %fusion.131 = (bf16[512,128]{0,1:T(8,128)(2,1)}, f32[512,128]{0,1:T(8,128)S(1)}) fusion(bf16[1,1,512,128]{2,3,1,0:T(8,128)(2,1)} %copy.250, f32[]{:T(128)} %bitcast.25, f32[128,512]{1,0:T(8,128)} %fusion.117, bf16[512,512]{1,0:T(8,128)(2,1)S(1)} %copy-done.2, f32[128,512]{0,1:T(8,128)S(1)} %copy-done.4, f32[128,512]{0,1:T(8,128)S(1)} %copy-done.3, ...), kind=kOutput, calls=%fused_computation.195 | convolution fusion | flops 67895296 | bytes 2359300 | tf_op jit(solution)/shard_map/dot_general | solution.py:31
  134.1 2.2 %fusion.35 = (bf16[512,128]{0,1:T(8,128)(2,1)S(1)}, bf16[512,128]{0,1:T(8,128)(2,1)S(1)}) fusion(bf16[1,1,512,128]{2,3,1,0:T(8,128)(2,1)} %copy.254, bf16[1,1,512,128]{2,3,1,0:T(8,128)(2,1)} %copy.253, bf16[1,1,512,128]{2,3,1,0:T(8,128)(2,1)} %copy.250, f32[512,128]{0,1:T(8,128)S(1)} %get-tuple-element.37, f32[]{:T(128)} %bitcast.25, ...), kind=kOutput, calls=%fused_computation.86 | convolution fusion | flops 68419584 | bytes 2752516 | tf_op jit(solution)/shard_map/dot_general | solution.py:31
  140.8 15.3 %all_to_all.25 = bf16[8,2,2,16,512]{4,3,2,1,0:T(8,128)(2,1)S(1)} all-to-all(bf16[8,2,2,16,512]{4,3,2,1,0:T(8,128)(2,1)S(1)} %copy_bitcast_fusion.1), channel_id=1, replica_groups=mesh['dp'=8,'ctx'=64] {'dp'}, dimensions={0} | all-to-all | bytes 1048576 | tf_op jit(solution)/shard_map/all_to_all | solution.py:74
  156.6 1.0 convert_element_type.330
  157.6 10.0 %all-to-all-start.4 = ((bf16[64,4,128]{2,1,0:T(4,128)(2,1)}), bf16[64,4,128]{2,1,0:T(4,128)(2,1)S(1)}, u32[]{:S(2)}, u32[]{:S(2)}) async-start(bf16[64,4,128]{2,1,0:T(4,128)(2,1)} %convert_element_type.330), calls=%async_computation.4 | async-start | bytes 131072 | tf_op jit(solution)/shard_map/all_to_all | solution.py:74
  168.7 13.4 %all-to-all-done.4 = bf16[64,4,128]{2,1,0:T(4,128)(2,1)S(1)} async-done(((bf16[64,4,128]{2,1,0:T(4,128)(2,1)}), bf16[64,4,128]{2,1,0:T(4,128)(2,1)S(1)}, u32[]{:S(2)}, u32[]{:S(2)}) %all-to-all-start.4) | async-done | bytes 65568 | tf_op jit(solution)/shard_map/all_to_all | solution.py:74
  182.1 4.5 %all-to-all-start.2 = ((bf16[64,2,8,128]{3,2,1,0:T(8,128)(2,1)}), bf16[64,2,8,128]{3,2,1,0:T(8,128)(2,1)S(1)}, u32[]{:S(2)}, u32[]{:S(2)}) async-start(bf16[64,2,8,128]{3,2,1,0:T(8,128)(2,1)} %copy.209), calls=%async_computation.2 | async-start | bytes 524288 | tf_op jit(solution)/shard_map/all_to_all | solution.py:74
  186.7 4.5 %copy.229 = f32[2,4,16,2,64,2]{1,5,4,3,2,0:T(2,128)} copy(f32[2,4,16,2,64,2]{4,2,0,5,3,1:T(8,128)S(1)} %bitcast.288) | data formatting | bytes 262144 | tf_op jit(solution)/shard_map/convert_element_type | solution.py:103
  191.2 3.5 %copy.231 = f32[2,4,32,128]{3,2,1,0:T(8,128)} copy(f32[2,4,32,128]{1,3,2,0:T(8,128)} %bitcast.260) | data formatting | bytes 262144
  194.7 14.2 %all-to-all-done.2 = bf16[64,2,8,128]{3,2,1,0:T(8,128)(2,1)S(1)} async-done(((bf16[64,2,8,128]{3,2,1,0:T(8,128)(2,1)}), bf16[64,2,8,128]{3,2,1,0:T(8,128)(2,1)S(1)}, u32[]{:S(2)}, u32[]{:S(2)}) %all-to-all-start.2) | async-done | bytes 262176 | tf_op jit(solution)/shard_map/all_to_all | solution.py:74
  (138 shorter events, 19.1 us)
Async XLA Ops:
  0.6 1.2 copy-start
  0.6 23.0 %copy-start.37 = (bf16[1,1024,128]{2,1,0:T(8,128)(2,1)S(1)}, bf16[1,1024,128]{2,1,0:T(8,128)(2,1)}, u32[]{:S(2)}) copy-start(bf16[1,1024,128]{2,1,0:T(8,128)(2,1)} %param.11) | copy-start | bytes 786436
  5.6 32.5 %all-to-all-start.1 = ((bf16[64,4,128]{2,1,0:T(4,128)(2,1)}), bf16[64,4,128]{2,1,0:T(4,128)(2,1)S(1)}, u32[]{:S(2)}, u32[]{:S(2)}) async-start(bf16[64,4,128]{2,1,0:T(4,128)(2,1)} %copy.192), calls=%async_computation.1 | async-start | bytes 131072 | tf_op jit(solution)/shard_map/all_to_all | solution.py:74
  23.8 19.5 %copy-start.40 = (f32[128]{0:T(128)S(1)}, f32[128]{0:T(128)}, u32[]{:S(2)}) copy-start(f32[128]{0:T(128)} %param.15) | copy-start | bytes 1540
  27.4 61.2 %copy-start.2 = (bf16[512,512]{1,0:T(8,128)(2,1)S(1)}, bf16[512,512]{1,0:T(8,128)(2,1)}, u32[]{:S(2)}) copy-start(bf16[512,512]{1,0:T(8,128)(2,1)} %constant.52) | copy-start | bytes 1572868
  38.1 48.3 %all-to-all-start = ((bf16[64,3,2,8,128]{4,3,2,1,0:T(8,128)(2,1)}), bf16[64,3,2,8,128]{4,3,2,1,0:T(8,128)(2,1)}, u32[]{:S(2)}, u32[]{:S(2)}) async-start(bf16[64,3,2,8,128]{4,3,2,1,0:T(8,128)(2,1)} %copy.197), calls=%async_computation | async-start | bytes 1572864 | tf_op jit(solution)/shard_map/all_to_all | solution.py:74
  43.3 46.6 %copy-start.1 = (bf16[512,512]{1,0:T(8,128)(2,1)S(1)}, bf16[512,512]{1,0:T(8,128)(2,1)}, u32[]{:S(2)}) copy-start(bf16[512,512]{1,0:T(8,128)(2,1)} %constant.51) | copy-start | bytes 1572868
  45.2 46.0 %copy-start.4 = (f32[128,512]{0,1:T(8,128)S(1)}, f32[128,512]{0,1:T(8,128)}, u32[]{:S(2)}) copy-start(f32[128,512]{0,1:T(8,128)} %constant.54) | copy-start | bytes 786436
  45.2 46.0 %copy-start.6 = (f32[512,128]{1,0:T(8,128)S(1)}, f32[512,128]{1,0:T(8,128)}, u32[]{:S(2)}) copy-start(f32[512,128]{1,0:T(8,128)} %constant.41.clone) | copy-start | bytes 786436
  45.2 46.0 %copy-start.18 = (bf16[256,128]{1,0:T(8,128)(2,1)S(1)}, bf16[256,128]{1,0:T(8,128)(2,1)}, u32[]{:S(2)}) copy-start(bf16[256,128]{1,0:T(8,128)(2,1)} %constant.56) | copy-start | bytes 196612
  78.7 12.9 %copy-start.3 = (f32[128,512]{0,1:T(8,128)S(1)}, f32[128,512]{0,1:T(8,128)}, u32[]{:S(2)}) copy-start(f32[128,512]{0,1:T(8,128)} %constant.53) | copy-start | bytes 786436
  78.7 12.9 %copy-start.5 = (f32[512,128]{1,0:T(8,128)S(1)}, f32[512,128]{1,0:T(8,128)}, u32[]{:S(2)}) copy-start(f32[512,128]{1,0:T(8,128)} %constant.42.clone) | copy-start | bytes 786436
  78.7 12.9 %copy-start.17 = (bf16[256,128]{1,0:T(8,128)(2,1)S(1)}, bf16[256,128]{1,0:T(8,128)(2,1)}, u32[]{:S(2)}) copy-start(bf16[256,128]{1,0:T(8,128)(2,1)} %constant.58) | copy-start | bytes 196612
  87.7 4.1 %copy-start.7 = (bf16[64,3,2,8,128]{4,3,0,2,1:T(8,128)(2,1)}, bf16[64,3,2,8,128]{4,3,0,2,1:T(8,128)(2,1)S(1)}, u32[]{:S(2)}) copy-start(bf16[64,3,2,8,128]{4,3,0,2,1:T(8,128)(2,1)S(1)} %copy.261) | copy-start | bytes 2359300
  87.7 4.1 %copy-start.19 = (bf16[1,1,8,16,512]{4,3,1,0,2:T(8,128)(2,1)S(1)}, bf16[1,1,8,16,512]{4,3,1,0,2:T(8,128)(2,1)}, u32[]{:S(2)}) copy-start(bf16[1,1,8,16,512]{4,3,1,0,2:T(8,128)(2,1)} %get-tuple-element.26) | copy-start | bytes 393220
  87.7 4.1 %copy-start.21 = (bf16[1,1,8,16,512]{4,3,1,0,2:T(8,128)(2,1)S(1)}, bf16[1,1,8,16,512]{4,3,1,0,2:T(8,128)(2,1)}, u32[]{:S(2)}) copy-start(bf16[1,1,8,16,512]{4,3,1,0,2:T(8,128)(2,1)} %get-tuple-element.29) | copy-start | bytes 393220
  87.8 4.1 %copy-start.35 = (bf16[256,128]{1,0:T(8,128)(2,1)S(1)}, bf16[256,128]{1,0:T(8,128)(2,1)}, u32[]{:S(2)}) copy-start(bf16[256,128]{1,0:T(8,128)(2,1)} %constant.55) | copy-start | bytes 196612
  88.6 4.0 %copy-start.31 = (bf16[256,128]{1,0:T(8,128)(2,1)S(1)}, bf16[256,128]{1,0:T(8,128)(2,1)}, u32[]{:S(2)}) copy-start(bf16[256,128]{1,0:T(8,128)(2,1)} %constant.60) | copy-start | bytes 196612
  91.8 0.8 copy-start.9
  92.9 0.8 copy-start.28
  96.4 4.1 %copy-start.20 = (bf16[1,1,8,16,512]{4,3,1,0,2:T(8,128)(2,1)S(1)}, bf16[1,1,8,16,512]{4,3,1,0,2:T(8,128)(2,1)}, u32[]{:S(2)}) copy-start(bf16[1,1,8,16,512]{4,3,1,0,2:T(8,128)(2,1)} %get-tuple-element.26) | copy-start | bytes 393220
  96.4 4.1 %copy-start.22 = (bf16[1,1,8,16,512]{4,3,1,0,2:T(8,128)(2,1)S(1)}, bf16[1,1,8,16,512]{4,3,1,0,2:T(8,128)(2,1)}, u32[]{:S(2)}) copy-start(bf16[1,1,8,16,512]{4,3,1,0,2:T(8,128)(2,1)} %get-tuple-element.29) | copy-start | bytes 393220
  96.4 4.1 %copy-start.32 = (bf16[256,128]{1,0:T(8,128)(2,1)S(1)}, bf16[256,128]{1,0:T(8,128)(2,1)}, u32[]{:S(2)}) copy-start(bf16[256,128]{1,0:T(8,128)(2,1)} %constant.60) | copy-start | bytes 196612
  99.0 1.5 copy-start.11
  100.8 0.8 copy-start.30
  106.0 9.0 %copy-start.8 = (bf16[64,3,2,8,128]{4,3,0,2,1:T(8,128)(2,1)S(1)}, bf16[64,3,2,8,128]{4,3,0,2,1:T(8,128)(2,1)}, u32[]{:S(2)}) copy-start(bf16[64,3,2,8,128]{4,3,0,2,1:T(8,128)(2,1)} %copy-done.7) | copy-start | bytes 2359300
  114.0 4.1 %copy-start.36 = (bf16[256,128]{1,0:T(8,128)(2,1)S(1)}, bf16[256,128]{1,0:T(8,128)(2,1)}, u32[]{:S(2)}) copy-start(bf16[256,128]{1,0:T(8,128)(2,1)} %constant.55) | copy-start | bytes 196612
  115.0 3.9 %copy-start.33 = (bf16[256,128]{1,0:T(8,128)(2,1)S(1)}, bf16[256,128]{1,0:T(8,128)(2,1)}, u32[]{:S(2)}) copy-start(bf16[256,128]{1,0:T(8,128)(2,1)} %constant.60) | copy-start | bytes 196612
  118.1 0.8 copy-start.13
  119.2 0.8 copy-start.27
  122.7 3.8 %copy-start.34 = (bf16[256,128]{1,0:T(8,128)(2,1)S(1)}, bf16[256,128]{1,0:T(8,128)(2,1)}, u32[]{:S(2)}) copy-start(bf16[256,128]{1,0:T(8,128)(2,1)} %constant.60) | copy-start | bytes 196612
  125.3 1.2 copy-start.15
  126.8 0.8 copy-start.29
  131.2 6.4 %copy-start.25 = (f32[128,512]{0,1:T(8,128)S(1)}, f32[128,512]{0,1:T(8,128)}, u32[]{:S(2)}) copy-start(f32[128,512]{0,1:T(8,128)} %convolution_negate_fusion.7) | copy-start | bytes 786436
  131.2 6.4 %copy-start.26 = (f32[512,128]{1,0:T(8,128)S(1)}, f32[512,128]{1,0:T(8,128)}, u32[]{:S(2)}) copy-start(f32[512,128]{1,0:T(8,128)} %fusion.133) | copy-start | bytes 786436
  136.4 1.8 copy-start.23
  136.4 1.8 copy-start.24
  138.7 1.1 copy-start.10
  138.7 1.2 copy-start.12
  138.9 1.2 copy-start.14
  138.9 1.3 copy-start.16
  140.2 27.4 %copy-start.38 = (bf16[512,128]{0,1:T(8,128)(2,1)S(1)}, bf16[512,128]{0,1:T(8,128)(2,1)}, u32[]{:S(2)}) copy-start(bf16[512,128]{0,1:T(8,128)(2,1)} %get-tuple-element.38) | copy-start | bytes 393220
  140.5 27.3 %copy-start.39 = (bf16[512,128]{0,1:T(8,128)(2,1)S(1)}, bf16[512,128]{0,1:T(8,128)(2,1)}, u32[]{:S(2)}) copy-start(bf16[512,128]{0,1:T(8,128)(2,1)} %get-tuple-element.36) | copy-start | bytes 393220
  157.6 24.5 %all-to-all-start.4 = ((bf16[64,4,128]{2,1,0:T(4,128)(2,1)}), bf16[64,4,128]{2,1,0:T(4,128)(2,1)S(1)}, u32[]{:S(2)}, u32[]{:S(2)}) async-start(bf16[64,4,128]{2,1,0:T(4,128)(2,1)} %convert_element_type.330), calls=%async_computation.4 | async-start | bytes 131072 | tf_op jit(solution)/shard_map/all_to_all | solution.py:74
  182.1 26.8 %all-to-all-start.2 = ((bf16[64,2,8,128]{3,2,1,0:T(8,128)(2,1)}), bf16[64,2,8,128]{3,2,1,0:T(8,128)(2,1)S(1)}, u32[]{:S(2)}, u32[]{:S(2)}) async-start(bf16[64,2,8,128]{3,2,1,0:T(8,128)(2,1)} %copy.209), calls=%async_computation.2 | async-start | bytes 524288 | tf_op jit(solution)/shard_map/all_to_all | solution.py:74

commit v2 on v1

v2 whole, which is shorter than its diff:
```python
import numpy as np
import jax
import jax.numpy as jnp
from jax import lax
from jax.experimental import pallas as pl
from jax.experimental.pallas import tpu as pltpu
from jax.sharding import PartitionSpec as P

M1 = 512
M2 = 128
N = M1 * M2
SMART = 2.0
BF = jnp.bfloat16
F32 = jnp.float32
MESH = pl.DeviceIdType.MESH
NC = 64
ND = 8


def trig(rows, cols, period):
    turn = (np.arange(rows)[:, None] * np.arange(cols)[None, :]) % period
    angle = turn * (2.0 * np.pi / period)
    return np.cos(angle), np.sin(angle)


def tables():
    c1, s1 = trig(M1, M1, M1)
    tc, ts = trig(M1, M2, N)
    c2, s2 = trig(M2, M2, M2)
    wf = np.block([[c2, s2], [-s2, c2]])
    wi = np.block([[c2, -s2], [s2, c2]])

    def blocks(t):
        return t.reshape(4, 128, M2).transpose(0, 2, 1)

    values = (c1, s1, tc, ts, blocks(tc), blocks(ts), wf, wi)
    kinds = (BF, BF, F32, F32, F32, F32, BF, BF)
    return [jnp.asarray(v.astype(np.float32)).astype(k) for v, k in zip(values, kinds)]


def nn(a, b):
    return lax.dot_general(a, b, (((1,), (0,)), ((), ())), preferred_element_type=F32)


def nt(a, b):
    return lax.dot_general(a, b, (((1,), (1,)), ((), ())), preferred_element_type=F32)


def half(x, j):
    return x[:, j * 128:(j + 1) * 128]


def kernel(sig, fmsg, gain, *refs):
    tabs_h, refs = refs[:8], refs[8:]
    out, gout = refs[:2]
    (rsig, rf, fpiece, filt, x, spec, y, sre, sim, osend, gacc, gsend, grecv, zsend) = refs[2:16]
    tabs, refs = refs[16:24], refs[24:]
    tsem, ssem, rsem = refs
    c1, s1, tc, ts, tct, tst, wf, wi = tabs
    me = lax.axis_index("ctx")
    mine = lax.axis_index("dp")
    barrier = pltpu.get_barrier_semaphore()

    def peer(a, count, here):
        step = lax.div(a + 1, 2)
        off = jnp.where(lax.rem(a, 2) == 1, step, count - step)
        return lax.rem(here + off, count)

    def greet(axis, count, here):
        def one(a, _):
            pl.semaphore_signal(
                barrier, inc=1, device_id={axis: peer(a, count, here)}, device_id_type=MESH
            )
            return 0

        lax.fori_loop(1, count, one, 0)

    greet("ctx", NC, me)
    greet("dp", ND, mine)
    loads = [pltpu.make_async_copy(h, v, tsem.at[i]) for i, (h, v) in enumerate(zip(tabs_h, tabs))]
    for load in loads:
        load.start()
    pl.semaphore_wait(barrier, NC + ND - 2)

    def scatter(axis, count, here, src, dst, k):
        pltpu.make_async_copy(src(here), dst(here), rsem.at[k]).start()

        def one(a, _):
            to = peer(a, count, here)
            pltpu.make_async_remote_copy(
                src_ref=src(to),
                dst_ref=dst(here),
                send_sem=ssem.at[k],
                recv_sem=rsem.at[k],
                device_id={axis: to},
                device_id_type=MESH,
            ).start()
            return 0

        lax.fori_loop(1, count, one, 0)

    def arrived(ref, k):
        pltpu.make_async_copy(ref, ref, rsem.at[k]).wait()

    def sent(ref, k):
        pltpu.make_async_copy(ref, ref, ssem.at[k]).wait()

    scatter("ctx", NC, me, lambda r: fmsg.at[r], lambda r: rf.at[r], 3)
    for i in range(3):
        scatter("ctx", NC, me, lambda r, i=i: sig.at[i, r], lambda r, i=i: rsig.at[i, r], i)

    arrived(rf, 3)
    ftab = rf[...].astype(F32).reshape(256, 128)
    for hi in range(2):
        turned = ftab[hi * 128:(hi + 1) * 128].T.astype(BF)
        for h in range(2):
            fpiece[2 * h + hi] = turned[h * 64:(h + 1) * 64].reshape(2, 2, 16, 128)
    scatter("dp", ND, mine, lambda d: fpiece, lambda d: filt.at[d], 4)
    for load in loads:
        load.wait()
    gains = jnp.concatenate([gain[0], gain[1]], 1)

    def gather(i, rows16, j):
        return rsig[i, rows16, j].astype(F32).reshape(128, 128)

    def take(i):
        arrived(rsig.at[i], i)

        def one(b, _):
            for j in range(2):
                x[i, pl.ds(b * 128, 128), j * 128:(j + 1) * 128] = gather(
                    i, pl.ds(b * 16, 16), j
                ).astype(BF)
            return 0

        lax.fori_loop(0, 4, one, 0)

    def forward(i, emit):
        def one(b, _):
            rows = pl.ds(b * 128, 128)
            a = nn(c1[rows, :], x[i])
            m = nn(s1[rows, :], x[i])
            co, si = tc[rows, :], ts[rows, :]
            for j in range(2):
                aj, mj = half(a, j), half(m, j)
                t = jnp.concatenate([aj * co - mj * si, -(mj * co + aj * si)], 1).astype(BF)
                emit(b, j, nt(wf[...], t))
            return 0

        lax.fori_loop(0, 4, one, 0)

    def keep(i):
        def emit(b, j, value):
            spec[i, j, b] = value

        return emit

    def convolve(i, emit):
        def one(b, _):
            for j in range(2):
                re, im = spec[i, j, b, :128], spec[i, j, b, 128:]
                fr = filt[:, b, j, 0].reshape(128, 128).astype(F32)
                fi = filt[:, b, j, 1].reshape(128, 128).astype(F32)
                prod = jnp.concatenate([fr * re - fi * im, fr * im + fi * re], 0).astype(BF)
                v = nn(wi[...], prod)
                vr, vi = v[:128], v[128:]
                co, si = tct[b], tst[b]
                lanes = pl.ds(pl.multiple_of(b * 128, 128), 128)
                sre[j * 128:(j + 1) * 128, lanes] = (vr * co - vi * si).astype(BF)
                sim[j * 128:(j + 1) * 128, lanes] = (vi * co + vr * si).astype(BF)
            return 0

        lax.fori_loop(0, 4, one, 0)

        def two(b, _):
            rows = pl.ds(b * 128, 128)
            conv = (nt(c1[rows, :], sre[...]) - nt(s1[rows, :], sim[...])) * (1.0 / N)
            conv = conv.astype(BF).astype(F32)
            wide = x[i, rows].astype(F32)
            emit(b, rows, wide, wide * conv + gains * wide)
            return 0

        lax.fori_loop(0, 4, two, 0)

    def clean(b, rows, wide, value):
        y[rows] = value
        for j in range(2):
            osend[pl.ds(b * 16, 16), j] = half(value, j).reshape(16, 8, 128).astype(BF)

    def shifted(b, rows, wide, value):
        gap = SMART * (value - y[rows])
        y[rows] = gap
        x[2, rows] = (wide * gap).astype(BF)

    def grad_term(err, i, j, b):
        er, ei = err[:128], err[128:]
        re, im = spec[i, j, b, :128], spec[i, j, b, 128:]
        return jnp.concatenate([er * re + ei * im, ei * re - er * im], 0)

    def first(b, j, err):
        gacc[j, b] = grad_term(err, 1, j, b)

    def second(b, j, err):
        g = ((gacc[j, b] + grad_term(err, 0, j, b)) * (1.0 / N)).astype(BF)
        for p in range(2):
            gsend[b, :, j, p] = g[p * 128:(p + 1) * 128].reshape(8, 16, 128)

    take(0)
    forward(0, keep(0))
    arrived(filt, 4)
    convolve(0, clean)
    scatter("ctx", NC, me, lambda r: osend.at[r], lambda r: out.at[r], 5)
    take(1)
    forward(1, keep(1))
    convolve(1, shifted)
    forward(2, first)
    arrived(rsig.at[2], 2)

    def errors(b, _):
        rows = pl.ds(b * 128, 128)
        for j in range(2):
            lanes = slice(j * 128, (j + 1) * 128)
            cot = gather(2, pl.ds(b * 16, 16), j)
            x[2, rows, lanes] = (x[0, rows, lanes].astype(F32) * (cot - y[rows, lanes])).astype(BF)
        return 0

    lax.fori_loop(0, 4, errors, 0)
    forward(2, second)
    scatter("dp", ND, mine, lambda d: gsend.at[:, d], lambda d: grecv.at[d], 6)
    arrived(grecv, 6)
    total = grecv[0].astype(F32)
    for d in range(1, ND):
        total = total + grecv[d].astype(F32)
    total = total.reshape(4, 64, 128)
    for hi in range(2):
        turned = jnp.concatenate([total[hi], total[2 + hi]], 0).T
        zsend[hi * 32:(hi + 1) * 32] = turned.reshape(32, 4, 128).astype(BF)
    scatter("ctx", NC, me, lambda r: zsend.at[r], lambda r: gout.at[r], 7)
    arrived(out, 5)
    arrived(gout, 7)
    for i in range(3):
        sent(rsig.at[i, pl.ds(0, NC - 1)], i)
    sent(rf.at[pl.ds(0, NC - 1)], 3)
    sent(filt.at[pl.ds(0, ND - 1)], 4)
    sent(osend.at[pl.ds(0, NC - 1)], 5)
    sent(grecv.at[pl.ds(0, ND - 1)], 6)
    sent(zsend.at[pl.ds(0, NC - 1)], 7)


def exchange(sig, part, gains):
    tabs = tables()
    vmem = pl.BlockSpec(memory_space=pltpu.VMEM)
    hbm = pl.BlockSpec(memory_space=pl.ANY)
    return pl.pallas_call(
        kernel,
        out_shape=(
            jax.ShapeDtypeStruct((NC, 2, 8, 128), BF),
            jax.ShapeDtypeStruct((NC, 4, 128), BF),
        ),
        in_specs=[vmem, vmem, vmem] + [hbm] * 8,
        out_specs=(hbm, hbm),
        scratch_shapes=[
            pltpu.VMEM((3, NC, 2, 8, 128), BF),
            pltpu.VMEM((NC, 4, 128), BF),
            pltpu.VMEM((4, 2, 2, 16, 128), BF),
            pltpu.VMEM((ND, 4, 2, 2, 16, 128), BF),
            pltpu.VMEM((3, M1, 256), BF),
            pltpu.VMEM((2, 2, 4, 256, 128), F32),
            pltpu.VMEM((M1, 256), F32),
            pltpu.VMEM((256, M1), BF),
            pltpu.VMEM((256, M1), BF),
            pltpu.VMEM((NC, 2, 8, 128), BF),
            pltpu.VMEM((2, 4, 256, 128), F32),
            pltpu.VMEM((4, ND, 2, 2, 16, 128), BF),
            pltpu.VMEM((ND, 4, 2, 2, 16, 128), BF),
            pltpu.VMEM((NC, 4, 128), BF),
        ]
        + [pltpu.VMEM(t.shape, t.dtype) for t in tabs]
        + [
            pltpu.SemaphoreType.DMA((8,)),
            pltpu.SemaphoreType.DMA((8,)),
            pltpu.SemaphoreType.DMA((8,)),
        ],
        compiler_params=pltpu.CompilerParams(
            collective_id=0, has_side_effects=True, vmem_limit_bytes=48 * 1024 * 1024
        ),
    )(sig, part, gains, *tabs)


def body(embeds, perturb, cotangent, filter_spectrum, skip_gain):
    d = lax.axis_index("dp")
    q = lax.axis_index("ctx")
    e = embeds[0]
    s = (e.astype(F32) + perturb[0].astype(F32)).astype(BF)
    sig = jnp.stack([e, s, cotangent[0]], 0).reshape(3, 8, 128, NC, 2).transpose(0, 3, 4, 1, 2)
    part = lax.dynamic_slice_in_dim(filter_spectrum, d * 32, 32, 2).astype(BF)
    part = part.reshape(2, 4, 16, 2, NC, 2).transpose(4, 1, 3, 5, 0, 2).reshape(NC, 4, 128)
    gains = lax.dynamic_slice_in_dim(skip_gain, 2 * q, 2, 0)
    gains = jnp.broadcast_to(gains[:, None, None], (2, 1, 128))
    out, g = exchange(sig, part, gains)
    out = out.transpose(2, 3, 0, 1).reshape(1, 1024, 128)
    g = g.reshape(NC, 4, 2, 2, 2, 16)
    g = g.transpose(4, 1, 5, 2, 0, 3).reshape(2, 4, 32, 128).astype(F32)
    return out, g


def solution(mesh):
    return jax.shard_map(
        body,
        mesh=mesh,
        in_specs=(
            P("dp", "ctx", None),
            P("dp", "ctx", None),
            P("dp", "ctx", None),
            P(None, "ctx", None, None),
            P(),
        ),
        out_specs=(P("dp", "ctx", None), P(None, "ctx", "dp", None)),
        check_vma=False,
    )
```

time: 211 us -> 114 us (0.54)
  Pallas kernels: 0 us -> 81.7 us
  blocking collectives: 47.9 us -> 0 us
  waiting for transfers between devices: 46.1 us -> 0 us
  starting transfers between devices: 37.8 us -> 0 us
  matrix products: 36.4 us -> 0 us
  local copies, waits for them, and re-layouts: 38.1 us -> 28.7 us
    pallas_call x0 -> x1, Pallas kernels: none -> 81.7 us  [exchange(): pl.pallas_call(kernel, out_shape=(jax.ShapeDtypeStruct((NC, 2, 8, 128), B...]
    all_to_all x4 -> x0, waiting for transfers between devices: 46.1 us -> none  [a2a(): return lax.all_to_all(x, axis, split_axis=0, concat_axis=0, tiled=True)]
    all_to_all x4 -> x0, starting transfers between devices: 37.8 us -> none  [a2a(): return lax.all_to_all(x, axis, split_axis=0, concat_axis=0, tiled=True)]
    dot_general x48 -> x0, matrix products: 36.4 us -> none  [dot(): lax.dot_general(a, b, (((ca,), (cb,)), ((), ())), preferred_element_type=...]
    all_gather x1 -> x0, blocking collectives: 32.6 us -> none  [body(): filt = lax.all_gather(part, 'dp', axis=2).reshape(2, 2 * M2, M1)]
    all_to_all x1 -> x0, blocking collectives: 15.3 us -> none  [a2a(): return lax.all_to_all(x, axis, split_axis=0, concat_axis=0, tiled=True)]
    unnamed x95 -> x27, local copies, waits for them, and re-layouts: 21.3 us -> 12.9 us
    transpose x3 -> x1, local copies, waits for them, and re-layouts: 3.59 us -> 6.05 us  [body(): part.reshape(2, 4, 16, 2, NC, 2).transpose(4, 1, 3, 5, 0, 2)]
  transfers between devices with their start and end apart: 4 -> 0, of which waited for: 4 -> 0; matrix products, arithmetic and copies ran while one was open for 7% -> 0% of each run, Pallas kernels for 0% -> 0%
where the time goes in v2:
time: 114 us; the launch traced here: 113 us
  Pallas kernels  81.7 us (72%)
  local copies, waits for them, and re-layouts  28.7 us (25%)
  other arithmetic  2.22 us (2%)
    pallas_call x1, Pallas kernels, exchange(): pl.pallas_call(kernel, out_shape=(jax.ShapeDtypeStruct((NC, 2, 8, 128), B...  81.7 us
    unnamed x27, local copies, waits for them, and re-layouts  12.9 us
    transpose x1, local copies, waits for them, and re-layouts, body(): part.reshape(2, 4, 16, 2, NC, 2).transpose(4, 1, 3, 5, 0, 2)  6.05 us
    convert_element_type x2, local copies, waits for them, and re-layouts, body(): g = g.transpose(4, 1, 5, 2, 0, 3).reshape(2, 4, 32, 128).astype(F32)  4.74 us

profile of v2, /device:TPU:1, one launch (start us, length us, event | category | flops | bytes accessed | tf_op | source)
XLA Modules:
  0.0 113.4 jit_solution(11287818345547284987)
XLA Ops:
  0.6 0.0 copy-start
  0.7 0.8 dynamic_slice.7
  1.5 0.1 broadcast_in_dim.2.gain
  1.5 0.3 copy-done
  1.9 1.1 add_convert_fusion
  3.0 0.1 copy.22
  3.1 0.8 copy.32
  3.9 0.0 copy-start.1
  3.9 0.0 copy-start.2
  3.9 0.0 copy-start.3
  3.9 0.0 copy-start.4
  3.9 1.2 %copy.23 = bf16[1,1024,128]{1,2,0:T(8,128)(2,1)S(1)} copy(bf16[1,1024,128]{2,1,0:T(8,128)(2,1)} %param.15) | data formatting | bytes 524288 | tf_op args[2]
  5.1 0.8 copy.33
  5.9 1.1 copy.21
  7.0 1.1 maximum_bitcast_fusion.sig
  8.2 1.9 %copy.24 = bf16[2,4,32,128]{1,3,2,0:T(8,128)(2,1)} copy(bf16[2,4,32,128]{3,2,1,0:T(8,128)(2,1)S(1)} %dynamic-slice_convert_fusion) | data formatting | bytes 131072 | tf_op jit(solution)/shard_map/convert_element_type | solution.py:296
  10.0 6.0 %copy.25 = bf16[64,4,2,2,2,16]{0,5,4,3,2,1:T(8,128)(2,1)} copy(bf16[64,4,2,2,2,16]{1,3,0,2,5,4:T(2,128)(2,1)} %bitcast.35) | data formatting | bytes 131072 | tf_op jit(solution)/shard_map/transpose | solution.py:297
  16.1 1.0 copy.26.fmsg
  17.1 0.0 copy-done.1
  17.1 0.0 copy-done.2
  17.1 0.0 copy-done.3
  17.1 0.0 copy-done.4
  17.1 0.0 copy-start.5
  17.2 0.9 copy-done.5
  18.1 0.0 copy-start.6
  18.1 0.9 copy-done.6
  19.1 0.0 copy-start.8
  19.1 0.9 copy-done.8
  20.0 0.0 copy-start.9
  20.0 0.9 copy-done.9
  20.9 81.7 %shard_map.140 = (bf16[64,2,8,128]{3,2,1,0:T(8,128)(2,1)S(1)}, bf16[64,4,128]{2,1,0:T(4,128)(2,1)S(1)}) custom-call(bf16[3,64,2,8,128]{4,3,2,1,0:T(8,128)(2,1)S(1)} %maximum_bitcast_fusion.sig, bf16[64,4,128]{2,1,0:T(4,128)(2,1)S(1)} %copy.26.fmsg, f32[2,1,128]{2,1,0:T(1,128)S(1)} %broadcast_in_dim.2.gain, bf16[512,512]{1,0:T(8,128)(2,1)S(1)} %copy-done.2, ...), custom_call_target="tpu_custom_call" | custom-call | tf_op jit(solution)/shard_map/pallas_call | solution.py:254
  102.6 0.0 copy-start.7
  102.6 0.7 copy-done.7
  103.3 1.1 reshape.28
  104.4 0.8 copy.29
  105.2 0.1 copy.27
  105.3 4.6 %copy.28 = f32[2,4,16,2,64,2]{1,5,4,3,2,0:T(2,128)} copy(f32[2,4,16,2,64,2]{4,2,0,5,3,1:T(8,128)S(1)} %bitcast.36) | data formatting | bytes 262144 | tf_op jit(solution)/shard_map/convert_element_type | solution.py:303
  109.9 3.5 %copy.30 = f32[2,4,32,128]{3,2,1,0:T(8,128)} copy(f32[2,4,32,128]{1,3,2,0:T(8,128)} %bitcast.34) | data formatting | bytes 262144
  (2 shorter events, 0.1 us)
Async XLA Ops:
  0.6 1.2 %copy-start = (f32[2,4,256,128]{3,2,1,0:T(8,128)S(1)}, f32[2,4,256,128]{3,2,1,0:T(8,128)}, u32[]{:S(2)}) copy-start(f32[2,4,256,128]{3,2,1,0:T(8,128)} %param.16) | copy-start | bytes 3145732
  3.9 13.2 %copy-start.1 = (bf16[512,512]{1,0:T(8,128)(2,1)S(1)}, bf16[512,512]{1,0:T(8,128)(2,1)}, u32[]{:S(2)}) copy-start(bf16[512,512]{1,0:T(8,128)(2,1)} %constant.48.refs_1_) | copy-start | bytes 1572868
  3.9 13.2 %copy-start.2 = (bf16[512,512]{1,0:T(8,128)(2,1)S(1)}, bf16[512,512]{1,0:T(8,128)(2,1)}, u32[]{:S(2)}) copy-start(bf16[512,512]{1,0:T(8,128)(2,1)} %constant.47.refs_0_) | copy-start | bytes 1572868
  3.9 13.2 %copy-start.3 = (f32[4,128,128]{2,1,0:T(8,128)S(1)}, f32[4,128,128]{2,1,0:T(8,128)}, u32[]{:S(2)}) copy-start(f32[4,128,128]{2,1,0:T(8,128)} %constant.40.clone.refs_5_) | copy-start | bytes 786436
  3.9 13.2 %copy-start.4 = (f32[4,128,128]{2,1,0:T(8,128)S(1)}, f32[4,128,128]{2,1,0:T(8,128)}, u32[]{:S(2)}) copy-start(f32[4,128,128]{2,1,0:T(8,128)} %constant.39.clone.refs_4_) | copy-start | bytes 786436
  17.1 1.0 copy-start.5
  18.1 0.9 copy-start.6
  19.1 0.9 copy-start.8
  20.0 0.9 copy-start.9
  102.6 0.7 copy-start.7

commit v3 on v2

--- a/solution.py
+++ b/solution.py
@@ -15,6 +15,7 @@
 MESH = pl.DeviceIdType.MESH
 NC = 64
 ND = 8
+VMEM_BYTES = 60 * 1024 * 1024
 
 
 def trig(rows, cols, period):
@@ -50,18 +51,30 @@
     return x[:, j * 128:(j + 1) * 128]
 
 
-def kernel(sig, fmsg, gain, *refs):
+def kernel(emb, per, cot, fil, gain, *refs):
     tabs_h, refs = refs[:8], refs[8:]
     out, gout = refs[:2]
-    (rsig, rf, fpiece, filt, x, spec, y, sre, sim, osend, gacc, gsend, grecv, zsend) = refs[2:16]
-    tabs, refs = refs[16:24], refs[24:]
+    (sig, fmsg, oraw, graw) = refs[2:6]
+    (rsig, rf, fpiece, filt, x, spec, y, sre, sim, osend, gacc, gsend, grecv, zsend) = refs[6:20]
+    (ein, pin, cin, fin, stage, small) = refs[20:26]
+    tabs, refs = refs[26:34], refs[34:]
     tsem, ssem, rsem = refs
     c1, s1, tc, ts, tct, tst, wf, wi = tabs
     me = lax.axis_index("ctx")
     mine = lax.axis_index("dp")
+    inputs = (
+        (fil.at[:, :, pl.ds(pl.multiple_of(mine * 32, 32), 32), :], fin),
+        (emb.at[0], ein),
+        (per.at[0], pin),
+        (cot.at[0], cin),
+    )
+    copies = [pltpu.make_async_copy(h, v, tsem.at[i]) for i, (h, v) in enumerate(inputs)]
+    for copy in copies:
+        copy.start()
     barrier = pltpu.get_barrier_semaphore()
 
     def peer(a, count, here):
+        a = count - a
         step = lax.div(a + 1, 2)
         off = jnp.where(lax.rem(a, 2) == 1, step, count - step)
         return lax.rem(here + off, count)
@@ -77,10 +90,20 @@
 
     greet("ctx", NC, me)
     greet("dp", ND, mine)
-    loads = [pltpu.make_async_copy(h, v, tsem.at[i]) for i, (h, v) in enumerate(zip(tabs_h, tabs))]
+    loads = [
+        pltpu.make_async_copy(h, v, tsem.at[4 + i]) for i, (h, v) in enumerate(zip(tabs_h, tabs))
+    ]
     for load in loads:
         load.start()
-    pl.semaphore_wait(barrier, NC + ND - 2)
+    row = lax.broadcasted_iota(jnp.int32, (128, 128), 0)
+    col = lax.broadcasted_iota(jnp.int32, (128, 128), 1)
+    eye = jnp.where(row == col, 1.0, 0.0).astype(BF)
+    picks = [jnp.where(col[:NC] == 2 * row[:NC] + j, 1.0, 0.0).astype(BF) for j in range(2)]
+
+    def pack(i, source):
+        for t in range(8):
+            stage[:, t, :] = nt(eye, source[t * 128:(t + 1) * 128, :])
+        sig[i] = stage[...].astype(BF).reshape(NC, 2, 8, 128)
 
     def scatter(axis, count, here, src, dst, k):
         pltpu.make_async_copy(src(here), dst(here), rsem.at[k]).start()
@@ -105,20 +128,64 @@
     def sent(ref, k):
         pltpu.make_async_copy(ref, ref, ssem.at[k]).wait()
 
-    scatter("ctx", NC, me, lambda r: fmsg.at[r], lambda r: rf.at[r], 3)
-    for i in range(3):
-        scatter("ctx", NC, me, lambda r, i=i: sig.at[i, r], lambda r, i=i: rsig.at[i, r], i)
-
-    arrived(rf, 3)
+    def gone(i):
+        sent(rsig.at[i, pl.ds(0, NC - 1)], i)
+
+    def send(i):
+        scatter("ctx", NC, me, lambda r: sig.at[i, r], lambda r: rsig.at[i, r], i)
+
+    with jax.named_scope("pack_filter"):
+        copies[0].wait()
+        both = jnp.concatenate(picks, 1)
+        for i in range(4):
+            z = jnp.concatenate(
+                [fin[p, i, pl.ds(h, 16, stride=2), :] for h in range(2) for p in range(2)], 0
+            ).astype(BF)
+            none = jnp.zeros_like(z)
+            wide = jnp.concatenate(
+                [jnp.concatenate([z, none], 1), jnp.concatenate([none, z], 1)], 0
+            )
+            small[:, i, :] = nt(both, wide)
+        fmsg[...] = small[...].astype(BF)
+    with jax.named_scope("pack_embeds"):
+        copies[1].wait()
+        pack(0, ein)
+    with jax.named_scope("greeted"):
+        pl.semaphore_wait(barrier, NC + ND - 2)
+    with jax.named_scope("send_filter_embeds"):
+        scatter("ctx", NC, me, lambda r: fmsg.at[r], lambda r: rf.at[r], 3)
+        send(0)
+    with jax.named_scope("pack_others"):
+        copies[2].wait()
+        pin[...] = (ein[...].astype(F32) + pin[...].astype(F32)).astype(BF)
+        pack(1, pin)
+        copies[3].wait()
+        pack(2, cin)
+    with jax.named_scope("embeds_sent"):
+        gone(0)
+    send(1)
+    with jax.named_scope("wait_filter"):
+        arrived(rf, 3)
     ftab = rf[...].astype(F32).reshape(256, 128)
     for hi in range(2):
         turned = ftab[hi * 128:(hi + 1) * 128].T.astype(BF)
-        for h in range(2):
-            fpiece[2 * h + hi] = turned[h * 64:(h + 1) * 64].reshape(2, 2, 16, 128)
+        for j in range(2):
+            for h in range(2):
+                base = j * 64 + h * 32
+                fpiece[2 * h + hi, j] = turned[base:base + 32].reshape(2, 16, 128)
     scatter("dp", ND, mine, lambda d: fpiece, lambda d: filt.at[d], 4)
     for load in loads:
         load.wait()
-    gains = jnp.concatenate([gain[0], gain[1]], 1)
+    lane = lax.broadcasted_iota(jnp.int32, (1, 128), 1)
+    gains = jnp.concatenate(
+        [
+            jnp.broadcast_to(
+                jnp.sum(jnp.where(lane == 2 * me + j, gain[...], 0.0), 1, keepdims=True), (1, 128)
+            )
+            for j in range(2)
+        ],
+        1,
+    )
 
     def gather(i, rows16, j):
         return rsig[i, rows16, j].astype(F32).reshape(128, 128)
@@ -135,7 +202,7 @@
 
         lax.fori_loop(0, 4, one, 0)
 
-    def forward(i, emit):
+    def forward(i, emit, done=None):
         def one(b, _):
             rows = pl.ds(b * 128, 128)
             a = nn(c1[rows, :], x[i])
@@ -145,6 +212,8 @@
                 aj, mj = half(a, j), half(m, j)
                 t = jnp.concatenate([aj * co - mj * si, -(mj * co + aj * si)], 1).astype(BF)
                 emit(b, j, nt(wf[...], t))
+            if done is not None:
+                done(b)
             return 0
 
         lax.fori_loop(0, 4, one, 0)
@@ -205,16 +274,34 @@
         for p in range(2):
             gsend[b, :, j, p] = g[p * 128:(p + 1) * 128].reshape(8, 16, 128)
 
-    take(0)
-    forward(0, keep(0))
-    arrived(filt, 4)
-    convolve(0, clean)
-    scatter("ctx", NC, me, lambda r: osend.at[r], lambda r: out.at[r], 5)
-    take(1)
-    forward(1, keep(1))
-    convolve(1, shifted)
-    forward(2, first)
-    arrived(rsig.at[2], 2)
+    def spread(b):
+        scatter("dp", ND, mine, lambda d: gsend.at[b, d], lambda d: grecv.at[d, b], 6)
+
+    with jax.named_scope("wait_embeds"):
+        take(0)
+    with jax.named_scope("forward_embeds"):
+        forward(0, keep(0))
+    with jax.named_scope("shifted_sent"):
+        gone(1)
+    send(2)
+    with jax.named_scope("wait_filter_dp"):
+        arrived(filt, 4)
+    with jax.named_scope("convolve_embeds"):
+        convolve(0, clean)
+    with jax.named_scope("wait_shifted"):
+        take(1)
+    with jax.named_scope("forward_shifted"):
+        forward(1, keep(1))
+    with jax.named_scope("convolve_shifted"):
+        convolve(1, shifted)
+    with jax.named_scope("forward_err_shifted"):
+        forward(2, first)
+    with jax.named_scope("cotangent_sent"):
+        gone(2)
+    with jax.named_scope("send_out"):
+        scatter("ctx", NC, me, lambda r: osend.at[r], lambda r: oraw.at[r], 5)
+    with jax.named_scope("wait_cotangent"):
+        arrived(rsig.at[2], 2)
 
     def errors(b, _):
         rows = pl.ds(b * 128, 128)
@@ -224,22 +311,36 @@
             x[2, rows, lanes] = (x[0, rows, lanes].astype(F32) * (cot - y[rows, lanes])).astype(BF)
         return 0
 
-    lax.fori_loop(0, 4, errors, 0)
-    forward(2, second)
-    scatter("dp", ND, mine, lambda d: gsend.at[:, d], lambda d: grecv.at[d], 6)
-    arrived(grecv, 6)
+    with jax.named_scope("errors"):
+        lax.fori_loop(0, 4, errors, 0)
+        forward(2, second, spread)
+    with jax.named_scope("wait_terms"):
+        arrived(grecv, 6)
     total = grecv[0].astype(F32)
     for d in range(1, ND):
         total = total + grecv[d].astype(F32)
-    total = total.reshape(4, 64, 128)
     for hi in range(2):
-        turned = jnp.concatenate([total[hi], total[2 + hi]], 0).T
+        turned = jnp.concatenate(
+            [total[2 * h + hi, j].reshape(32, 128) for j in range(2) for h in range(2)], 0
+        ).T
         zsend[hi * 32:(hi + 1) * 32] = turned.reshape(32, 4, 128).astype(BF)
-    scatter("ctx", NC, me, lambda r: zsend.at[r], lambda r: gout.at[r], 7)
-    arrived(out, 5)
-    arrived(gout, 7)
-    for i in range(3):
-        sent(rsig.at[i, pl.ds(0, NC - 1)], i)
+    with jax.named_scope("send_gradient"):
+        scatter("ctx", NC, me, lambda r: zsend.at[r], lambda r: graw.at[r], 7)
+    with jax.named_scope("wait_out"):
+        arrived(oraw, 5)
+    stage[...] = oraw[...].astype(F32).reshape(128, 8, 128)
+    for t in range(8):
+        out[0, t * 128:(t + 1) * 128, :] = nt(eye, stage[:, t, :].astype(BF)).astype(BF)
+    with jax.named_scope("wait_gradient"):
+        arrived(graw, 7)
+    small[...] = graw[...].astype(F32)
+    for i in range(4):
+        turned = small[:, i, :].T.astype(BF)
+        res = nn(turned[:64], picks[0]) + nn(turned[64:], picks[1])
+        for h in range(2):
+            for p in range(2):
+                base = h * 32 + p * 16
+                gout[p, i, pl.ds(h, 16, stride=2), :] = res[base:base + 16]
     sent(rf.at[pl.ds(0, NC - 1)], 3)
     sent(filt.at[pl.ds(0, ND - 1)], 4)
     sent(osend.at[pl.ds(0, NC - 1)], 5)
@@ -247,19 +348,23 @@
     sent(zsend.at[pl.ds(0, NC - 1)], 7)
 
 
-def exchange(sig, part, gains):
+def body(embeds, perturb, cotangent, filter_spectrum, skip_gain):
     tabs = tables()
     vmem = pl.BlockSpec(memory_space=pltpu.VMEM)
-    hbm = pl.BlockSpec(memory_space=pl.ANY)
+    hbm = pl.BlockSpec(memory_space=pltpu.HBM)
     return pl.pallas_call(
         kernel,
         out_shape=(
-            jax.ShapeDtypeStruct((NC, 2, 8, 128), BF),
-            jax.ShapeDtypeStruct((NC, 4, 128), BF),
+            jax.ShapeDtypeStruct((1, 1024, 128), BF),
+            jax.ShapeDtypeStruct((2, 4, 32, 128), F32),
         ),
-        in_specs=[vmem, vmem, vmem] + [hbm] * 8,
-        out_specs=(hbm, hbm),
+        in_specs=[hbm] * 4 + [vmem] + [hbm] * 8,
+        out_specs=(vmem, vmem),
         scratch_shapes=[
+            pltpu.VMEM((3, NC, 2, 8, 128), BF),
+            pltpu.VMEM((NC, 4, 128), BF),
+            pltpu.VMEM((NC, 2, 8, 128), BF),
+            pltpu.VMEM((NC, 4, 128), BF),
             pltpu.VMEM((3, NC, 2, 8, 128), BF),
             pltpu.VMEM((NC, 4, 128), BF),
             pltpu.VMEM((4, 2, 2, 16, 128), BF),
@@ -274,34 +379,23 @@
             pltpu.VMEM((4, ND, 2, 2, 16, 128), BF),
             pltpu.VMEM((ND, 4, 2, 2, 16, 128), BF),
             pltpu.VMEM((NC, 4, 128), BF),
+            pltpu.VMEM((1024, 128), BF),
+            pltpu.VMEM((1024, 128), BF),
+            pltpu.VMEM((1024, 128), BF),
+            pltpu.VMEM((2, 4, 32, 128), F32),
+            pltpu.VMEM((128, 8, 128), F32),
+            pltpu.VMEM((NC, 4, 128), F32),
         ]
         + [pltpu.VMEM(t.shape, t.dtype) for t in tabs]
         + [
-            pltpu.SemaphoreType.DMA((8,)),
+            pltpu.SemaphoreType.DMA((12,)),
             pltpu.SemaphoreType.DMA((8,)),
             pltpu.SemaphoreType.DMA((8,)),
         ],
         compiler_params=pltpu.CompilerParams(
-            collective_id=0, has_side_effects=True, vmem_limit_bytes=48 * 1024 * 1024
+            collective_id=0, has_side_effects=True, vmem_limit_bytes=VMEM_BYTES
         ),
-    )(sig, part, gains, *tabs)
-
-
-def body(embeds, perturb, cotangent, filter_spectrum, skip_gain):
-    d = lax.axis_index("dp")
-    q = lax.axis_index("ctx")
-    e = embeds[0]
-    s = (e.astype(F32) + perturb[0].astype(F32)).astype(BF)
-    sig = jnp.stack([e, s, cotangent[0]], 0).reshape(3, 8, 128, NC, 2).transpose(0, 3, 4, 1, 2)
-    part = lax.dynamic_slice_in_dim(filter_spectrum, d * 32, 32, 2).astype(BF)
-    part = part.reshape(2, 4, 16, 2, NC, 2).transpose(4, 1, 3, 5, 0, 2).reshape(NC, 4, 128)
-    gains = lax.dynamic_slice_in_dim(skip_gain, 2 * q, 2, 0)
-    gains = jnp.broadcast_to(gains[:, None, None], (2, 1, 128))
-    out, g = exchange(sig, part, gains)
-    out = out.transpose(2, 3, 0, 1).reshape(1, 1024, 128)
-    g = g.reshape(NC, 4, 2, 2, 2, 16)
-    g = g.transpose(4, 1, 5, 2, 0, 3).reshape(2, 4, 32, 128).astype(F32)
-    return out, g
+    )(embeds, perturb, cotangent, filter_spectrum, skip_gain.reshape(1, 128), *tabs)
 
 
 def solution(mesh):

time: 114 us -> 83.6 us (0.73)
  local copies, waits for them, and re-layouts: 28.7 us -> 2.36 us
  other arithmetic: 2.22 us -> 0 us
  Pallas kernels: 81.7 us -> 80.5 us
    unnamed x27 -> x4, local copies, waits for them, and re-layouts: 12.9 us -> 2.36 us
    convert_element_type x5 -> x0, local copies, waits for them, and re-layouts: 6.8 us -> none  [the longest x2 4.74 us: body(): g = g.transpose(4, 1, 5, 2, 0, 3).reshape(2, 4, 32, 128).astype(F32)]
    transpose x1 -> x0, local copies, waits for them, and re-layouts: 6.05 us -> none  [body(): part.reshape(2, 4, 16, 2, NC, 2).transpose(4, 1, 3, 5, 0, 2)]
    reshape x2 -> x0, local copies, waits for them, and re-layouts: 2.07 us -> none  [the longest x1 1.06 us: body(): out = out.transpose(2, 3, 0, 1).reshape(1, 1024, 128)]
    pallas_call x1, Pallas kernels: 81.7 us -> 80.5 us  [body(): pl.pallas_call(kernel, out_shape=(jax.ShapeDtypeStruct((1, 1024, 128), BF...]
where the time goes in v3:
time: 83.6 us; the launch traced here: 83.5 us
  Pallas kernels  80.5 us (96%)
  local copies, waits for them, and re-layouts  2.36 us (3%)
    pallas_call x1, Pallas kernels, body(): pl.pallas_call(kernel, out_shape=(jax.ShapeDtypeStruct((1, 1024, 128), BF...  80.5 us
    unnamed x4, local copies, waits for them, and re-layouts  2.36 us

profile of v3, /device:TPU:1, one launch (start us, length us, event | category | flops | bytes accessed | tf_op | source)
XLA Modules:
  0.0 83.5 jit_solution(6613234862785377873)
XLA Ops:
  0.6 80.5 %shard_map.140 = (bf16[1,1024,128]{2,1,0:T(8,128)(2,1)}, f32[2,4,32,128]{3,2,1,0:T(8,128)}) custom-call(bf16[1,1024,128]{2,1,0:T(8,128)(2,1)} %emb.1, bf16[1,1024,128]{2,1,0:T(8,128)(2,1)} %per.1, bf16[1,1024,128]{2,1,0:T(8,128)(2,1)} %cot.1, f32[2,4,256,128]{3,2,1,0:T(8,128)} %fil.1, f32[1,128]{1,0:T(1,128)} %bitcast.1, bf16[512,512]{1,0:T(8,128)(2,1)} %constant.28.refs_0_, ...), custom_call_target="tpu_custom_call" | custom-call | tf_op jit(solution)/shard_map/pallas_call | solution.py:355
  81.1 0.0 copy-start
  81.1 1.7 %copy.17 = bf16[1,1024,128]{2,1,0:T(8,128)(2,1)} copy(bf16[1,1024,128]{2,1,0:T(8,128)(2,1)} %get-tuple-element.4) | data formatting | bytes 524288
  82.8 0.0 copy-done
  82.8 0.7 copy.18
Async XLA Ops:
  81.1 1.7 %copy-start = (f32[2,4,32,128]{3,2,1,0:T(8,128)S(1)}, f32[2,4,32,128]{3,2,1,0:T(8,128)}, u32[]{:S(2)}) copy-start(f32[2,4,32,128]{3,2,1,0:T(8,128)} %get-tuple-element.5) | copy-start | bytes 393220

commit v4 on v3

--- a/solution.py
+++ b/solution.py
@@ -15,6 +15,7 @@
 MESH = pl.DeviceIdType.MESH
 NC = 64
 ND = 8
+GROUP = 2
 VMEM_BYTES = 60 * 1024 * 1024
 
 
@@ -74,15 +75,14 @@
     barrier = pltpu.get_barrier_semaphore()
 
     def peer(a, count, here):
-        a = count - a
-        step = lax.div(a + 1, 2)
-        off = jnp.where(lax.rem(a, 2) == 1, step, count - step)
-        return lax.rem(here + off, count)
+        back = count - a
+        step = (back + 1) // 2
+        return (here + jnp.where(back % 2 == 1, step, count - step)) & (count - 1)
 
     def greet(axis, count, here):
         def one(a, _):
             pl.semaphore_signal(
-                barrier, inc=1, device_id={axis: peer(a, count, here)}, device_id_type=MESH
+                barrier, inc=1, device_id={axis: (here + a) & (count - 1)}, device_id_type=MESH
             )
             return 0
 
@@ -103,7 +103,9 @@
     def pack(i, source):
         for t in range(8):
             stage[:, t, :] = nt(eye, source[t * 128:(t + 1) * 128, :])
-        sig[i] = stage[...].astype(BF).reshape(NC, 2, 8, 128)
+        turned = stage[...].astype(BF).reshape(NC, 2, 8, 128)
+        for j in range(2):
+            sig[i, j] = turned[:, j]
 
     def scatter(axis, count, here, src, dst, k):
         pltpu.make_async_copy(src(here), dst(here), rsem.at[k]).start()
@@ -128,11 +130,11 @@
     def sent(ref, k):
         pltpu.make_async_copy(ref, ref, ssem.at[k]).wait()
 
-    def gone(i):
-        sent(rsig.at[i, pl.ds(0, NC - 1)], i)
-
-    def send(i):
-        scatter("ctx", NC, me, lambda r: sig.at[i, r], lambda r: rsig.at[i, r], i)
+    def gone(i, j):
+        sent(rsig.at[i, j, pl.ds(0, NC - 1)], 2 * i + j)
+
+    def send(i, j):
+        scatter("ctx", NC, me, lambda r: sig.at[i, j, r], lambda r: rsig.at[i, j, r], 2 * i + j)
 
     with jax.named_scope("pack_filter"):
         copies[0].wait()
@@ -153,8 +155,9 @@
     with jax.named_scope("greeted"):
         pl.semaphore_wait(barrier, NC + ND - 2)
     with jax.named_scope("send_filter_embeds"):
-        scatter("ctx", NC, me, lambda r: fmsg.at[r], lambda r: rf.at[r], 3)
-        send(0)
+        scatter("ctx", NC, me, lambda r: fmsg.at[r], lambda r: rf.at[r], 6)
+        send(0, 0)
+        send(0, 1)
     with jax.named_scope("pack_others"):
         copies[2].wait()
         pin[...] = (ein[...].astype(F32) + pin[...].astype(F32)).astype(BF)
@@ -162,10 +165,10 @@
         copies[3].wait()
         pack(2, cin)
     with jax.named_scope("embeds_sent"):
-        gone(0)
-    send(1)
+        gone(0, 0)
+    send(1, 0)
     with jax.named_scope("wait_filter"):
-        arrived(rf, 3)
+        arrived(rf, 6)
     ftab = rf[...].astype(F32).reshape(256, 128)
     for hi in range(2):
         turned = ftab[hi * 128:(hi + 1) * 128].T.astype(BF)
@@ -173,7 +176,10 @@
             for h in range(2):
                 base = j * 64 + h * 32
                 fpiece[2 * h + hi, j] = turned[base:base + 32].reshape(2, 16, 128)
-    scatter("dp", ND, mine, lambda d: fpiece, lambda d: filt.at[d], 4)
+    scatter("dp", ND, mine, lambda d: fpiece, lambda d: filt.at[d], 7)
+    with jax.named_scope("embeds_sent_2"):
+        gone(0, 1)
+    send(1, 1)
     for load in loads:
         load.wait()
     lane = lax.broadcasted_iota(jnp.int32, (1, 128), 1)
@@ -187,11 +193,16 @@
         1,
     )
 
+    def blocks(step):
+        for b in range(4):
+            step(b, 0)
+
     def gather(i, rows16, j):
-        return rsig[i, rows16, j].astype(F32).reshape(128, 128)
+        return rsig[i, j, rows16].astype(F32).reshape(128, 128)
 
     def take(i):
-        arrived(rsig.at[i], i)
+        for j in range(2):
+            arrived(rsig.at[i, j], 2 * i + j)
 
         def one(b, _):
             for j in range(2):
@@ -200,23 +211,25 @@
                 ).astype(BF)
             return 0
 
-        lax.fori_loop(0, 4, one, 0)
-
-    def forward(i, emit, done=None):
+        blocks(one)
+
+    def forward(i, emit, done=None, js=(0, 1)):
+        lanes = slice(js[0] * 128, js[-1] * 128 + 128)
+
         def one(b, _):
             rows = pl.ds(b * 128, 128)
-            a = nn(c1[rows, :], x[i])
-            m = nn(s1[rows, :], x[i])
+            a = nn(c1[rows, :], x[i, :, lanes])
+            m = nn(s1[rows, :], x[i, :, lanes])
             co, si = tc[rows, :], ts[rows, :]
-            for j in range(2):
-                aj, mj = half(a, j), half(m, j)
+            for k, j in enumerate(js):
+                aj, mj = half(a, k), half(m, k)
                 t = jnp.concatenate([aj * co - mj * si, -(mj * co + aj * si)], 1).astype(BF)
                 emit(b, j, nt(wf[...], t))
             if done is not None:
                 done(b)
             return 0
 
-        lax.fori_loop(0, 4, one, 0)
+        blocks(one)
 
     def keep(i):
         def emit(b, j, value):
@@ -239,7 +252,7 @@
                 sim[j * 128:(j + 1) * 128, lanes] = (vi * co + vr * si).astype(BF)
             return 0
 
-        lax.fori_loop(0, 4, one, 0)
+        blocks(one)
 
         def two(b, _):
             rows = pl.ds(b * 128, 128)
@@ -249,7 +262,7 @@
             emit(b, rows, wide, wide * conv + gains * wide)
             return 0
 
-        lax.fori_loop(0, 4, two, 0)
+        blocks(two)
 
     def clean(b, rows, wide, value):
         y[rows] = value
@@ -272,22 +285,37 @@
     def second(b, j, err):
         g = ((gacc[j, b] + grad_term(err, 0, j, b)) * (1.0 / N)).astype(BF)
         for p in range(2):
-            gsend[b, :, j, p] = g[p * 128:(p + 1) * 128].reshape(8, 16, 128)
-
-    def spread(b):
-        scatter("dp", ND, mine, lambda d: gsend.at[b, d], lambda d: grecv.at[d, b], 6)
+            gsend[j, :, b, p] = g[p * 128:(p + 1) * 128].reshape(8, 16, 128)
+
+    def spread(j):
+        def done(b):
+            if b % GROUP == GROUP - 1:
+                rows = pl.ds(b + 1 - GROUP, GROUP)
+                scatter(
+                    "dp",
+                    ND,
+                    mine,
+                    lambda d: gsend.at[j, d, rows],
+                    lambda d: grecv.at[d, j, rows],
+                    9,
+                )
+
+        return done
 
     with jax.named_scope("wait_embeds"):
         take(0)
     with jax.named_scope("forward_embeds"):
         forward(0, keep(0))
     with jax.named_scope("shifted_sent"):
-        gone(1)
-    send(2)
+        gone(1, 0)
+    send(2, 0)
     with jax.named_scope("wait_filter_dp"):
-        arrived(filt, 4)
+        arrived(filt, 7)
     with jax.named_scope("convolve_embeds"):
         convolve(0, clean)
+    with jax.named_scope("shifted_sent_2"):
+        gone(1, 1)
+    send(2, 1)
     with jax.named_scope("wait_shifted"):
         take(1)
     with jax.named_scope("forward_shifted"):
@@ -297,42 +325,47 @@
     with jax.named_scope("forward_err_shifted"):
         forward(2, first)
     with jax.named_scope("cotangent_sent"):
-        gone(2)
+        gone(2, 0)
+        gone(2, 1)
     with jax.named_scope("send_out"):
-        scatter("ctx", NC, me, lambda r: osend.at[r], lambda r: oraw.at[r], 5)
-    with jax.named_scope("wait_cotangent"):
-        arrived(rsig.at[2], 2)
-
-    def errors(b, _):
-        rows = pl.ds(b * 128, 128)
-        for j in range(2):
-            lanes = slice(j * 128, (j + 1) * 128)
+        scatter("ctx", NC, me, lambda r: osend.at[r], lambda r: oraw.at[r], 8)
+
+    def errors(j):
+        lanes = slice(j * 128, (j + 1) * 128)
+
+        def one(b, _):
+            rows = pl.ds(b * 128, 128)
             cot = gather(2, pl.ds(b * 16, 16), j)
             x[2, rows, lanes] = (x[0, rows, lanes].astype(F32) * (cot - y[rows, lanes])).astype(BF)
-        return 0
-
-    with jax.named_scope("errors"):
-        lax.fori_loop(0, 4, errors, 0)
-        forward(2, second, spread)
+            return 0
+
+        blocks(one)
+        forward(2, second, spread(j), (j,))
+
+    for j in range(2):
+        with jax.named_scope("wait_cotangent"):
+            arrived(rsig.at[2, j], 4 + j)
+        with jax.named_scope("errors"):
+            errors(j)
     with jax.named_scope("wait_terms"):
-        arrived(grecv, 6)
+        arrived(grecv, 9)
     total = grecv[0].astype(F32)
     for d in range(1, ND):
         total = total + grecv[d].astype(F32)
     for hi in range(2):
         turned = jnp.concatenate(
-            [total[2 * h + hi, j].reshape(32, 128) for j in range(2) for h in range(2)], 0
+            [total[j, 2 * h + hi].reshape(32, 128) for j in range(2) for h in range(2)], 0
         ).T
         zsend[hi * 32:(hi + 1) * 32] = turned.reshape(32, 4, 128).astype(BF)
     with jax.named_scope("send_gradient"):
-        scatter("ctx", NC, me, lambda r: zsend.at[r], lambda r: graw.at[r], 7)
+        scatter("ctx", NC, me, lambda r: zsend.at[r], lambda r: graw.at[r], 10)
     with jax.named_scope("wait_out"):
-        arrived(oraw, 5)
+        arrived(oraw, 8)
     stage[...] = oraw[...].astype(F32).reshape(128, 8, 128)
     for t in range(8):
         out[0, t * 128:(t + 1) * 128, :] = nt(eye, stage[:, t, :].astype(BF)).astype(BF)
     with jax.named_scope("wait_gradient"):
-        arrived(graw, 7)
+        arrived(graw, 10)
     small[...] = graw[...].astype(F32)
     for i in range(4):
         turned = small[:, i, :].T.astype(BF)
@@ -341,18 +374,30 @@
             for p in range(2):
                 base = h * 32 + p * 16
                 gout[p, i, pl.ds(h, 16, stride=2), :] = res[base:base + 16]
-    sent(rf.at[pl.ds(0, NC - 1)], 3)
-    sent(filt.at[pl.ds(0, ND - 1)], 4)
-    sent(osend.at[pl.ds(0, NC - 1)], 5)
-    sent(grecv.at[pl.ds(0, ND - 1)], 6)
-    sent(zsend.at[pl.ds(0, NC - 1)], 7)
+    sent(rf.at[pl.ds(0, NC - 1)], 6)
+    sent(filt.at[pl.ds(0, ND - 1)], 7)
+    sent(osend.at[pl.ds(0, NC - 1)], 8)
+    sent(grecv.at[pl.ds(0, ND - 1)], 9)
+    sent(zsend.at[pl.ds(0, NC - 1)], 10)
+
+
+def store(clean, grad, clean_out, grad_out, sem):
+    copies = [
+        pltpu.make_async_copy(clean, clean_out, sem.at[0]),
+        pltpu.make_async_copy(grad, grad_out, sem.at[1]),
+    ]
+    for copy in copies:
+        copy.start()
+    for copy in copies:
+        copy.wait()
 
 
 def body(embeds, perturb, cotangent, filter_spectrum, skip_gain):
     tabs = tables()
     vmem = pl.BlockSpec(memory_space=pltpu.VMEM)
     hbm = pl.BlockSpec(memory_space=pltpu.HBM)
-    return pl.pallas_call(
+    hbm_any = pl.BlockSpec(memory_space=pl.ANY)
+    results = pl.pallas_call(
         kernel,
         out_shape=(
             jax.ShapeDtypeStruct((1, 1024, 128), BF),
@@ -361,11 +406,11 @@
         in_specs=[hbm] * 4 + [vmem] + [hbm] * 8,
         out_specs=(vmem, vmem),
         scratch_shapes=[
-            pltpu.VMEM((3, NC, 2, 8, 128), BF),
+            pltpu.VMEM((3, 2, NC, 8, 128), BF),
             pltpu.VMEM((NC, 4, 128), BF),
             pltpu.VMEM((NC, 2, 8, 128), BF),
             pltpu.VMEM((NC, 4, 128), BF),
-            pltpu.VMEM((3, NC, 2, 8, 128), BF),
+            pltpu.VMEM((3, 2, NC, 8, 128), BF),
             pltpu.VMEM((NC, 4, 128), BF),
             pltpu.VMEM((4, 2, 2, 16, 128), BF),
             pltpu.VMEM((ND, 4, 2, 2, 16, 128), BF),
@@ -376,8 +421,8 @@
             pltpu.VMEM((256, M1), BF),
             pltpu.VMEM((NC, 2, 8, 128), BF),
             pltpu.VMEM((2, 4, 256, 128), F32),
-            pltpu.VMEM((4, ND, 2, 2, 16, 128), BF),
-            pltpu.VMEM((ND, 4, 2, 2, 16, 128), BF),
+            pltpu.VMEM((2, ND, 4, 2, 16, 128), BF),
+            pltpu.VMEM((ND, 2, 4, 2, 16, 128), BF),
             pltpu.VMEM((NC, 4, 128), BF),
             pltpu.VMEM((1024, 128), BF),
             pltpu.VMEM((1024, 128), BF),
@@ -389,13 +434,20 @@
         + [pltpu.VMEM(t.shape, t.dtype) for t in tabs]
         + [
             pltpu.SemaphoreType.DMA((12,)),
-            pltpu.SemaphoreType.DMA((8,)),
-            pltpu.SemaphoreType.DMA((8,)),
+            pltpu.SemaphoreType.DMA((11,)),
+            pltpu.SemaphoreType.DMA((11,)),
         ],
         compiler_params=pltpu.CompilerParams(
             collective_id=0, has_side_effects=True, vmem_limit_bytes=VMEM_BYTES
         ),
     )(embeds, perturb, cotangent, filter_spectrum, skip_gain.reshape(1, 128), *tabs)
+    return pl.pallas_call(
+        store,
+        out_shape=[jax.ShapeDtypeStruct(r.shape, r.dtype) for r in results],
+        in_specs=[hbm_any] * 2,
+        out_specs=[hbm_any] * 2,
+        scratch_shapes=[pltpu.SemaphoreType.DMA((2,))],
+    )(*results)
 
 
 def solution(mesh):

time: 83.6 us -> 90 us (1.077)
  Pallas kernels: 80.5 us -> 89.2 us
  local copies, waits for them, and re-layouts: 2.36 us -> 0 us
    pallas_call x0 -> x1, Pallas kernels: none -> 13 us  [body(): pl.pallas_call(store, out_shape=[jax.ShapeDtypeStruct(r.shape, r.dtype) f...]
    pallas_call x1, Pallas kernels: 80.5 us -> 76.2 us  [body(): pl.pallas_call(kernel, out_shape=(jax.ShapeDtypeStruct((1, 1024, 128), BF...]
    unnamed x4 -> x0, local copies, waits for them, and re-layouts: 2.36 us -> none
where the time goes in v4:
time: 90 us; the launch traced here: 89.8 us
  Pallas kernels  89.2 us (99%)
    pallas_call x1, Pallas kernels, body(): pl.pallas_call(kernel, out_shape=(jax.ShapeDtypeStruct((1, 1024, 128), BF...  76.2 us
    pallas_call x1, Pallas kernels, body(): pl.pallas_call(store, out_shape=[jax.ShapeDtypeStruct(r.shape, r.dtype) f...  13 us

profile of v4, /device:TPU:1, one launch (start us, length us, event | category | flops | bytes accessed | tf_op | source)
XLA Modules:
  0.0 89.8 jit_solution(13694563083892463491)
XLA Ops:
  0.6 76.2 %shard_map.140 = (bf16[1,1024,128]{2,1,0:T(8,128)(2,1)}, f32[2,4,32,128]{3,2,1,0:T(8,128)}) custom-call(bf16[1,1024,128]{2,1,0:T(8,128)(2,1)} %emb.1, bf16[1,1024,128]{2,1,0:T(8,128)(2,1)} %per.1, bf16[1,1024,128]{2,1,0:T(8,128)(2,1)} %cot.1, f32[2,4,256,128]{3,2,1,0:T(8,128)} %fil.1, f32[1,128]{1,0:T(1,128)} %bitcast.1, bf16[512,512]{1,0:T(8,128)(2,1)} %constant.28.refs_0_, ...), custom_call_target="tpu_custom_call" | custom-call | tf_op jit(solution)/shard_map/pallas_call | solution.py:400
  76.8 13.0 %shard_map.141 = (bf16[1,1024,128]{2,1,0:T(8,128)(2,1)}, f32[2,4,32,128]{3,2,1,0:T(8,128)}) custom-call(bf16[1,1024,128]{2,1,0:T(8,128)(2,1)} %get-tuple-element.4.clean, f32[2,4,32,128]{3,2,1,0:T(8,128)} %get-tuple-element.5.grad), custom_call_target="tpu_custom_call" | custom-call | tf_op jit(solution)/shard_map/pallas_call | solution.py:444

commit v5 on v4

--- a/solution.py
+++ b/solution.py
@@ -54,12 +54,12 @@
 
 def kernel(emb, per, cot, fil, gain, *refs):
     tabs_h, refs = refs[:8], refs[8:]
-    out, gout = refs[:2]
+    out_h, gout_h = refs[:2]
     (sig, fmsg, oraw, graw) = refs[2:6]
     (rsig, rf, fpiece, filt, x, spec, y, sre, sim, osend, gacc, gsend, grecv, zsend) = refs[6:20]
     (ein, pin, cin, fin, stage, small) = refs[20:26]
     tabs, refs = refs[26:34], refs[34:]
-    tsem, ssem, rsem = refs
+    out, gout, tsem, ssem, rsem = refs
     c1, s1, tc, ts, tct, tst, wf, wi = tabs
     me = lax.axis_index("ctx")
     mine = lax.axis_index("dp")
@@ -70,8 +70,6 @@
         (cot.at[0], cin),
     )
     copies = [pltpu.make_async_copy(h, v, tsem.at[i]) for i, (h, v) in enumerate(inputs)]
-    for copy in copies:
-        copy.start()
     barrier = pltpu.get_barrier_semaphore()
 
     def peer(a, count, here):
@@ -86,10 +84,14 @@
             )
             return 0
 
-        lax.fori_loop(1, count, one, 0)
-
-    greet("ctx", NC, me)
-    greet("dp", ND, mine)
+        for a in range(1, count):
+            one(a, 0)
+
+    with jax.named_scope("greet"):
+        greet("ctx", NC, me)
+        greet("dp", ND, mine)
+    for copy in copies:
+        copy.start()
     loads = [
         pltpu.make_async_copy(h, v, tsem.at[4 + i]) for i, (h, v) in enumerate(zip(tabs_h, tabs))
     ]
@@ -122,7 +124,7 @@
             ).start()
             return 0
 
-        lax.fori_loop(1, count, one, 0)
+        lax.fori_loop(1, count, one, 0, unroll=7)
 
     def arrived(ref, k):
         pltpu.make_async_copy(ref, ref, rsem.at[k]).wait()
@@ -297,7 +299,7 @@
                     mine,
                     lambda d: gsend.at[j, d, rows],
                     lambda d: grecv.at[d, j, rows],
-                    9,
+                    9 + j,
                 )
 
         return done
@@ -347,49 +349,76 @@
             arrived(rsig.at[2, j], 4 + j)
         with jax.named_scope("errors"):
             errors(j)
-    with jax.named_scope("wait_terms"):
-        arrived(grecv, 9)
-    total = grecv[0].astype(F32)
-    for d in range(1, ND):
-        total = total + grecv[d].astype(F32)
-    for hi in range(2):
-        turned = jnp.concatenate(
-            [total[j, 2 * h + hi].reshape(32, 128) for j in range(2) for h in range(2)], 0
-        ).T
-        zsend[hi * 32:(hi + 1) * 32] = turned.reshape(32, 4, 128).astype(BF)
-    with jax.named_scope("send_gradient"):
-        scatter("ctx", NC, me, lambda r: zsend.at[r], lambda r: graw.at[r], 10)
+    def pairs(z):
+        none = jnp.zeros_like(z)
+        wide = jnp.concatenate(
+            [jnp.concatenate([z, none], 1), jnp.concatenate([none, z], 1)], 0
+        )
+        return nt(both, wide)
+
+    for j in range(2):
+        with jax.named_scope("wait_terms"):
+            arrived(grecv.at[:, j], 9 + j)
+        total = grecv[0, j].astype(F32)
+        for d in range(1, ND):
+            total = total + grecv[d, j].astype(F32)
+        for hi in range(2):
+            z = jnp.concatenate([total[2 * h + hi].reshape(32, 128) for h in range(2)], 0)
+            zsend[j, hi * 32:(hi + 1) * 32] = pairs(z.astype(BF)).reshape(32, 2, 128).astype(BF)
+        with jax.named_scope("send_gradient"):
+            scatter(
+                "ctx", NC, me, lambda r, j=j: zsend.at[j, r], lambda r, j=j: graw.at[j, r], 11 + j
+            )
     with jax.named_scope("wait_out"):
         arrived(oraw, 8)
     stage[...] = oraw[...].astype(F32).reshape(128, 8, 128)
     for t in range(8):
         out[0, t * 128:(t + 1) * 128, :] = nt(eye, stage[:, t, :].astype(BF)).astype(BF)
+    stores = [
+        pltpu.make_async_copy(out, out_h, tsem.at[12]),
+        pltpu.make_async_copy(gout, gout_h, tsem.at[13]),
+    ]
+    stores[0].start()
     with jax.named_scope("wait_gradient"):
-        arrived(graw, 10)
-    small[...] = graw[...].astype(F32)
-    for i in range(4):
-        turned = small[:, i, :].T.astype(BF)
-        res = nn(turned[:64], picks[0]) + nn(turned[64:], picks[1])
-        for h in range(2):
-            for p in range(2):
-                base = h * 32 + p * 16
-                gout[p, i, pl.ds(h, 16, stride=2), :] = res[base:base + 16]
+        for j in range(2):
+            arrived(graw.at[j], 11 + j)
+    for i in range(2):
+        res = jnp.zeros((128, 128), F32)
+        for j in range(2):
+            small[:, 2 * j:2 * j + 2, :] = graw[j].astype(F32)
+            res = res + nn(small[:, 2 * j + i, :].T.astype(BF), picks[j])
+        for k in range(2):
+            for h in range(2):
+                for p in range(2):
+                    base = k * 64 + h * 32 + p * 16
+                    gout[p, 2 * i + k, pl.ds(h, 16, stride=2), :] = res[base:base + 16]
+    stores[1].start()
     sent(rf.at[pl.ds(0, NC - 1)], 6)
     sent(filt.at[pl.ds(0, ND - 1)], 7)
     sent(osend.at[pl.ds(0, NC - 1)], 8)
-    sent(grecv.at[pl.ds(0, ND - 1)], 9)
-    sent(zsend.at[pl.ds(0, NC - 1)], 10)
-
-
-def store(clean, grad, clean_out, grad_out, sem):
-    copies = [
-        pltpu.make_async_copy(clean, clean_out, sem.at[0]),
-        pltpu.make_async_copy(grad, grad_out, sem.at[1]),
+    for j in range(2):
+        sent(grecv.at[pl.ds(0, ND - 1), j], 9 + j)
+        sent(zsend.at[j, pl.ds(0, NC - 1)], 11 + j)
+    for copy in stores:
+        copy.wait()
+
+
+def store(clean, grad, clean_out, grad_out, clean_v, grad_v, sem):
+    loads = [
+        pltpu.make_async_copy(clean, clean_v, sem.at[0]),
+        pltpu.make_async_copy(grad, grad_v, sem.at[1]),
     ]
-    for copy in copies:
-        copy.start()
-    for copy in copies:
-        copy.wait()
+    stores = [
+        pltpu.make_async_copy(clean_v, clean_out, sem.at[2]),
+        pltpu.make_async_copy(grad_v, grad_out, sem.at[3]),
+    ]
+    for load in loads:
+        load.start()
+    for load, out in zip(loads, stores):
+        load.wait()
+        out.start()
+    for out in stores:
+        out.wait()
 
 
 def body(embeds, perturb, cotangent, filter_spectrum, skip_gain):
@@ -404,12 +433,12 @@
             jax.ShapeDtypeStruct((2, 4, 32, 128), F32),
         ),
         in_specs=[hbm] * 4 + [vmem] + [hbm] * 8,
-        out_specs=(vmem, vmem),
+        out_specs=(hbm_any, hbm_any),
         scratch_shapes=[
             pltpu.VMEM((3, 2, NC, 8, 128), BF),
             pltpu.VMEM((NC, 4, 128), BF),
             pltpu.VMEM((NC, 2, 8, 128), BF),
-            pltpu.VMEM((NC, 4, 128), BF),
+            pltpu.VMEM((2, NC, 2, 128), BF),
             pltpu.VMEM((3, 2, NC, 8, 128), BF),
             pltpu.VMEM((NC, 4, 128), BF),
             pltpu.VMEM((4, 2, 2, 16, 128), BF),
@@ -423,7 +452,7 @@
             pltpu.VMEM((2, 4, 256, 128), F32),
             pltpu.VMEM((2, ND, 4, 2, 16, 128), BF),
             pltpu.VMEM((ND, 2, 4, 2, 16, 128), BF),
-            pltpu.VMEM((NC, 4, 128), BF),
+            pltpu.VMEM((2, NC, 2, 128), BF),
             pltpu.VMEM((1024, 128), BF),
             pltpu.VMEM((1024, 128), BF),
             pltpu.VMEM((1024, 128), BF),
@@ -433,9 +462,11 @@
         ]
         + [pltpu.VMEM(t.shape, t.dtype) for t in tabs]
         + [
-            pltpu.SemaphoreType.DMA((12,)),
-            pltpu.SemaphoreType.DMA((11,)),
-            pltpu.SemaphoreType.DMA((11,)),
+            pltpu.VMEM((1, 1024, 128), BF),
+            pltpu.VMEM((2, 4, 32, 128), F32),
+            pltpu.SemaphoreType.DMA((14,)),
+            pltpu.SemaphoreType.DMA((13,)),
+            pltpu.SemaphoreType.DMA((13,)),
         ],
         compiler_params=pltpu.CompilerParams(
             collective_id=0, has_side_effects=True, vmem_limit_bytes=VMEM_BYTES
@@ -446,7 +477,8 @@
         out_shape=[jax.ShapeDtypeStruct(r.shape, r.dtype) for r in results],
         in_specs=[hbm_any] * 2,
         out_specs=[hbm_any] * 2,
-        scratch_shapes=[pltpu.SemaphoreType.DMA((2,))],
+        scratch_shapes=[pltpu.VMEM(r.shape, r.dtype) for r in results]
+        + [pltpu.SemaphoreType.DMA((4,))],
     )(*results)
 
 

time: 90 us -> 78.9 us (0.88)
  Pallas kernels: 89.2 us -> 78.1 us
    pallas_call x1, Pallas kernels: 13 us -> 1.73 us  [body(): pl.pallas_call(store, out_shape=[jax.ShapeDtypeStruct(r.shape, r.dtype) f...]
where the time goes in v5:
time: 78.9 us; the launch traced here: 78.8 us
  Pallas kernels  78.1 us (99%)
    pallas_call x1, Pallas kernels, body(): pl.pallas_call(kernel, out_shape=(jax.ShapeDtypeStruct((1, 1024, 128), BF...  76.4 us
    pallas_call x1, Pallas kernels, body(): pl.pallas_call(store, out_shape=[jax.ShapeDtypeStruct(r.shape, r.dtype) f...  1.73 us

profile of v5, /device:TPU:1, one launch (start us, length us, event | category | flops | bytes accessed | tf_op | source)
XLA Modules:
  0.0 78.8 jit_solution(12793589281583314419)
XLA Ops:
  0.6 76.4 %shard_map.140 = (bf16[1,1024,128]{2,1,0:T(8,128)(2,1)}, f32[2,4,32,128]{3,2,1,0:T(8,128)}) custom-call(bf16[1,1024,128]{2,1,0:T(8,128)(2,1)} %emb.1, bf16[1,1024,128]{2,1,0:T(8,128)(2,1)} %per.1, bf16[1,1024,128]{2,1,0:T(8,128)(2,1)} %cot.1, f32[2,4,256,128]{3,2,1,0:T(8,128)} %fil.1, f32[1,128]{1,0:T(1,128)} %bitcast.1, bf16[512,512]{1,0:T(8,128)(2,1)} %constant.28.refs_0_, ...), custom_call_target="tpu_custom_call" | custom-call | tf_op jit(solution)/shard_map/pallas_call | solution.py:429
  77.0 1.7 %shard_map.141 = (bf16[1,1024,128]{2,1,0:T(8,128)(2,1)}, f32[2,4,32,128]{3,2,1,0:T(8,128)}) custom-call(bf16[1,1024,128]{2,1,0:T(8,128)(2,1)} %get-tuple-element.4.clean, f32[2,4,32,128]{3,2,1,0:T(8,128)} %get-tuple-element.5.grad), custom_call_target="tpu_custom_call" | custom-call | tf_op jit(solution)/shard_map/pallas_call | solution.py:475

commit v6 on v5

--- a/solution.py
+++ b/solution.py
@@ -52,14 +52,14 @@
     return x[:, j * 128:(j + 1) * 128]
 
 
-def kernel(emb, per, cot, fil, gain, *refs):
+def kernel(emb, per, cot, fil, gain_h, *refs):
     tabs_h, refs = refs[:8], refs[8:]
-    out_h, gout_h = refs[:2]
-    (sig, fmsg, oraw, graw) = refs[2:6]
-    (rsig, rf, fpiece, filt, x, spec, y, sre, sim, osend, gacc, gsend, grecv, zsend) = refs[6:20]
-    (ein, pin, cin, fin, stage, small) = refs[20:26]
-    tabs, refs = refs[26:34], refs[34:]
-    out, gout, tsem, ssem, rsem = refs
+    out_h, graw = refs[:2]
+    (sig, fmsg, oraw) = refs[2:5]
+    (rsig, rf, fpiece, filt, x, spec, y, sre, sim, osend, gacc, gsend, grecv, zsend) = refs[5:19]
+    (ein, pin, cin, fin, stage, small) = refs[19:25]
+    tabs, refs = refs[25:33], refs[33:]
+    out, gain, tsem, ssem, rsem = refs
     c1, s1, tc, ts, tct, tst, wf, wi = tabs
     me = lax.axis_index("ctx")
     mine = lax.axis_index("dp")
@@ -68,6 +68,7 @@
         (emb.at[0], ein),
         (per.at[0], pin),
         (cot.at[0], cin),
+        (gain_h, gain),
     )
     copies = [pltpu.make_async_copy(h, v, tsem.at[i]) for i, (h, v) in enumerate(inputs)]
     barrier = pltpu.get_barrier_semaphore()
@@ -93,7 +94,7 @@
     for copy in copies:
         copy.start()
     loads = [
-        pltpu.make_async_copy(h, v, tsem.at[4 + i]) for i, (h, v) in enumerate(zip(tabs_h, tabs))
+        pltpu.make_async_copy(h, v, tsem.at[5 + i]) for i, (h, v) in enumerate(zip(tabs_h, tabs))
     ]
     for load in loads:
         load.start()
@@ -182,6 +183,7 @@
     with jax.named_scope("embeds_sent_2"):
         gone(0, 1)
     send(1, 1)
+    copies[4].wait()
     for load in loads:
         load.wait()
     lane = lax.broadcasted_iota(jnp.int32, (1, 128), 1)
@@ -374,71 +376,63 @@
     stage[...] = oraw[...].astype(F32).reshape(128, 8, 128)
     for t in range(8):
         out[0, t * 128:(t + 1) * 128, :] = nt(eye, stage[:, t, :].astype(BF)).astype(BF)
-    stores = [
-        pltpu.make_async_copy(out, out_h, tsem.at[12]),
-        pltpu.make_async_copy(gout, gout_h, tsem.at[13]),
-    ]
-    stores[0].start()
+    save = pltpu.make_async_copy(out, out_h, tsem.at[13])
+    save.start()
     with jax.named_scope("wait_gradient"):
         for j in range(2):
             arrived(graw.at[j], 11 + j)
-    for i in range(2):
-        res = jnp.zeros((128, 128), F32)
-        for j in range(2):
-            small[:, 2 * j:2 * j + 2, :] = graw[j].astype(F32)
-            res = res + nn(small[:, 2 * j + i, :].T.astype(BF), picks[j])
-        for k in range(2):
-            for h in range(2):
-                for p in range(2):
-                    base = k * 64 + h * 32 + p * 16
-                    gout[p, 2 * i + k, pl.ds(h, 16, stride=2), :] = res[base:base + 16]
-    stores[1].start()
     sent(rf.at[pl.ds(0, NC - 1)], 6)
     sent(filt.at[pl.ds(0, ND - 1)], 7)
     sent(osend.at[pl.ds(0, NC - 1)], 8)
     for j in range(2):
         sent(grecv.at[pl.ds(0, ND - 1), j], 9 + j)
         sent(zsend.at[j, pl.ds(0, NC - 1)], 11 + j)
-    for copy in stores:
-        copy.wait()
-
-
-def store(clean, grad, clean_out, grad_out, clean_v, grad_v, sem):
-    loads = [
-        pltpu.make_async_copy(clean, clean_v, sem.at[0]),
-        pltpu.make_async_copy(grad, grad_v, sem.at[1]),
-    ]
-    stores = [
-        pltpu.make_async_copy(clean_v, clean_out, sem.at[2]),
-        pltpu.make_async_copy(grad_v, grad_out, sem.at[3]),
-    ]
-    for load in loads:
-        load.start()
-    for load, out in zip(loads, stores):
-        load.wait()
-        out.start()
-    for out in stores:
-        out.wait()
+    save.wait()
+
+
+def store(clean, graw, clean_out, grad_out, clean_v, graw_v, small, grad_v, sem):
+    load_clean = pltpu.make_async_copy(clean, clean_v, sem.at[0])
+    load_grad = pltpu.make_async_copy(graw, graw_v, sem.at[1])
+    save_clean = pltpu.make_async_copy(clean_v, clean_out, sem.at[2])
+    save_grad = pltpu.make_async_copy(grad_v, grad_out, sem.at[3])
+    load_grad.start()
+    load_clean.start()
+    row = lax.broadcasted_iota(jnp.int32, (NC, 128), 0)
+    col = lax.broadcasted_iota(jnp.int32, (NC, 128), 1)
+    picks = [jnp.where(col == 2 * row + j, 1.0, 0.0).astype(BF) for j in range(2)]
+    load_grad.wait()
+    for j in range(2):
+        small[:, 2 * j:2 * j + 2, :] = graw_v[j].astype(F32)
+    load_clean.wait()
+    save_clean.start()
+    for i in range(2):
+        res = sum(nn(small[:, 2 * j + i, :].T.astype(BF), picks[j]) for j in range(2))
+        for k in range(2):
+            for h in range(2):
+                for p in range(2):
+                    base = k * 64 + h * 32 + p * 16
+                    grad_v[p, 2 * i + k, pl.ds(h, 16, stride=2), :] = res[base:base + 16]
+    save_grad.start()
+    save_clean.wait()
+    save_grad.wait()
 
 
 def body(embeds, perturb, cotangent, filter_spectrum, skip_gain):
     tabs = tables()
-    vmem = pl.BlockSpec(memory_space=pltpu.VMEM)
     hbm = pl.BlockSpec(memory_space=pltpu.HBM)
     hbm_any = pl.BlockSpec(memory_space=pl.ANY)
     results = pl.pallas_call(
         kernel,
         out_shape=(
             jax.ShapeDtypeStruct((1, 1024, 128), BF),
-            jax.ShapeDtypeStruct((2, 4, 32, 128), F32),
+            jax.ShapeDtypeStruct((2, NC, 2, 128), BF),
         ),
-        in_specs=[hbm] * 4 + [vmem] + [hbm] * 8,
+        in_specs=[hbm] * 13,
         out_specs=(hbm_any, hbm_any),
         scratch_shapes=[
             pltpu.VMEM((3, 2, NC, 8, 128), BF),
             pltpu.VMEM((NC, 4, 128), BF),
             pltpu.VMEM((NC, 2, 8, 128), BF),
-            pltpu.VMEM((2, NC, 2, 128), BF),
             pltpu.VMEM((3, 2, NC, 8, 128), BF),
             pltpu.VMEM((NC, 4, 128), BF),
             pltpu.VMEM((4, 2, 2, 16, 128), BF),
@@ -463,7 +457,7 @@
         + [pltpu.VMEM(t.shape, t.dtype) for t in tabs]
         + [
             pltpu.VMEM((1, 1024, 128), BF),
-            pltpu.VMEM((2, 4, 32, 128), F32),
+            pltpu.VMEM((1, 128), F32),
             pltpu.SemaphoreType.DMA((14,)),
             pltpu.SemaphoreType.DMA((13,)),
             pltpu.SemaphoreType.DMA((13,)),
@@ -474,11 +468,18 @@
     )(embeds, perturb, cotangent, filter_spectrum, skip_gain.reshape(1, 128), *tabs)
     return pl.pallas_call(
         store,
-        out_shape=[jax.ShapeDtypeStruct(r.shape, r.dtype) for r in results],
+        out_shape=[
+            jax.ShapeDtypeStruct((1, 1024, 128), BF),
+            jax.ShapeDtypeStruct((2, 4, 32, 128), F32),
+        ],
         in_specs=[hbm_any] * 2,
         out_specs=[hbm_any] * 2,
         scratch_shapes=[pltpu.VMEM(r.shape, r.dtype) for r in results]
-        + [pltpu.SemaphoreType.DMA((4,))],
+        + [
+            pltpu.VMEM((NC, 4, 128), F32),
+            pltpu.VMEM((2, 4, 32, 128), F32),
+            pltpu.SemaphoreType.DMA((4,)),
+        ],
     )(*results)
 
 

time: 78.9 us -> 77.8 us (0.986)
  Pallas kernels: 78.1 us -> 77 us
    pallas_call x1, Pallas kernels: 76.4 us -> 75.1 us  [body(): pl.pallas_call(kernel, out_shape=(jax.ShapeDtypeStruct((1, 1024, 128), BF...]
where the time goes in v6:
time: 77.8 us; the launch traced here: 77.7 us
  Pallas kernels  77 us (99%)
    pallas_call x1, Pallas kernels, body(): pl.pallas_call(kernel, out_shape=(jax.ShapeDtypeStruct((1, 1024, 128), BF...  75.1 us
    pallas_call x1, Pallas kernels, body(): pl.pallas_call(store, out_shape=[jax.ShapeDtypeStruct((1, 1024, 128), BF)...  1.96 us

profile of v6, /device:TPU:1, one launch (start us, length us, event | category | flops | bytes accessed | tf_op | source)
XLA Modules:
  0.0 77.7 jit_solution(14662314512770216659)
XLA Ops:
  0.6 75.1 %shard_map.140 = (bf16[1,1024,128]{2,1,0:T(8,128)(2,1)}, bf16[2,64,2,128]{3,2,1,0:T(2,128)(2,1)}) custom-call(bf16[1,1024,128]{2,1,0:T(8,128)(2,1)} %emb.1, bf16[1,1024,128]{2,1,0:T(8,128)(2,1)} %per.1, bf16[1,1024,128]{2,1,0:T(8,128)(2,1)} %cot.1, f32[2,4,256,128]{3,2,1,0:T(8,128)} %fil.1, f32[1,128]{1,0:T(1,128)} %bitcast.1, ...), custom_call_target="tpu_custom_call" | custom-call | tf_op jit(solution)/shard_map/pallas_call | solution.py:424
  75.7 2.0 %shard_map.141 = (bf16[1,1024,128]{2,1,0:T(8,128)(2,1)}, f32[2,4,32,128]{3,2,1,0:T(8,128)}) custom-call(bf16[1,1024,128]{2,1,0:T(8,128)(2,1)} %get-tuple-element.4.clean, bf16[2,64,2,128]{3,2,1,0:T(2,128)(2,1)} %get-tuple-element.5.graw), custom_call_target="tpu_custom_call" | custom-call | tf_op jit(solution)/shard_map/pallas_call | solution.py:469

commit v7 on v6

--- a/solution.py
+++ b/solution.py
@@ -328,11 +328,13 @@
         convolve(1, shifted)
     with jax.named_scope("forward_err_shifted"):
         forward(2, first)
-    with jax.named_scope("cotangent_sent"):
-        gone(2, 0)
-        gone(2, 1)
-    with jax.named_scope("send_out"):
-        scatter("ctx", NC, me, lambda r: osend.at[r], lambda r: oraw.at[r], 8)
+    def send_out(j):
+        with jax.named_scope("cotangent_sent"):
+            gone(2, j)
+        with jax.named_scope("send_out"):
+            scatter("ctx", NC, me, lambda r: osend.at[r, j], lambda r: oraw.at[r, j], 8 + 5 * j)
+
+    send_out(0)
 
     def errors(j):
         lanes = slice(j * 128, (j + 1) * 128)
@@ -351,6 +353,8 @@
             arrived(rsig.at[2, j], 4 + j)
         with jax.named_scope("errors"):
             errors(j)
+        if j == 0:
+            send_out(1)
     def pairs(z):
         none = jnp.zeros_like(z)
         wide = jnp.concatenate(
@@ -372,7 +376,8 @@
                 "ctx", NC, me, lambda r, j=j: zsend.at[j, r], lambda r, j=j: graw.at[j, r], 11 + j
             )
     with jax.named_scope("wait_out"):
-        arrived(oraw, 8)
+        for j in range(2):
+            arrived(oraw.at[:, j], 8 + 5 * j)
     stage[...] = oraw[...].astype(F32).reshape(128, 8, 128)
     for t in range(8):
         out[0, t * 128:(t + 1) * 128, :] = nt(eye, stage[:, t, :].astype(BF)).astype(BF)
@@ -383,7 +388,8 @@
             arrived(graw.at[j], 11 + j)
     sent(rf.at[pl.ds(0, NC - 1)], 6)
     sent(filt.at[pl.ds(0, ND - 1)], 7)
-    sent(osend.at[pl.ds(0, NC - 1)], 8)
+    for j in range(2):
+        sent(osend.at[pl.ds(0, NC - 1), j], 8 + 5 * j)
     for j in range(2):
         sent(grecv.at[pl.ds(0, ND - 1), j], 9 + j)
         sent(zsend.at[j, pl.ds(0, NC - 1)], 11 + j)
@@ -459,8 +465,8 @@
             pltpu.VMEM((1, 1024, 128), BF),
             pltpu.VMEM((1, 128), F32),
             pltpu.SemaphoreType.DMA((14,)),
-            pltpu.SemaphoreType.DMA((13,)),
-            pltpu.SemaphoreType.DMA((13,)),
+            pltpu.SemaphoreType.DMA((14,)),
+            pltpu.SemaphoreType.DMA((14,)),
         ],
         compiler_params=pltpu.CompilerParams(
             collective_id=0, has_side_effects=True, vmem_limit_bytes=VMEM_BYTES

time: 77.8 us -> 77.8 us (level)
  no operation moved by 1% of the time
where the time goes in v7:
time: 77.8 us; the launch traced here: 77.7 us
  Pallas kernels  77 us (99%)
    pallas_call x1, Pallas kernels, body(): pl.pallas_call(kernel, out_shape=(jax.ShapeDtypeStruct((1, 1024, 128), BF...  75.1 us
    pallas_call x1, Pallas kernels, body(): pl.pallas_call(store, out_shape=[jax.ShapeDtypeStruct((1, 1024, 128), BF)...  1.96 us

profile of v7, /device:TPU:1, one launch (start us, length us, event | category | flops | bytes accessed | tf_op | source)
XLA Modules:
  0.0 77.7 jit_solution(18024286004420356132)
XLA Ops:
  0.6 75.1 %shard_map.140 = (bf16[1,1024,128]{2,1,0:T(8,128)(2,1)}, bf16[2,64,2,128]{3,2,1,0:T(2,128)(2,1)}) custom-call(bf16[1,1024,128]{2,1,0:T(8,128)(2,1)} %emb.1, bf16[1,1024,128]{2,1,0:T(8,128)(2,1)} %per.1, bf16[1,1024,128]{2,1,0:T(8,128)(2,1)} %cot.1, f32[2,4,256,128]{3,2,1,0:T(8,128)} %fil.1, f32[1,128]{1,0:T(1,128)} %bitcast.1, ...), custom_call_target="tpu_custom_call" | custom-call | tf_op jit(solution)/shard_map/pallas_call | solution.py:430
  75.7 2.0 %shard_map.141 = (bf16[1,1024,128]{2,1,0:T(8,128)(2,1)}, f32[2,4,32,128]{3,2,1,0:T(8,128)}) custom-call(bf16[1,1024,128]{2,1,0:T(8,128)(2,1)} %get-tuple-element.4.clean, bf16[2,64,2,128]{3,2,1,0:T(2,128)(2,1)} %get-tuple-element.5.graw), custom_call_target="tpu_custom_call" | custom-call | tf_op jit(solution)/shard_map/pallas_call | solution.py:475
